TPU v7x, 256 devices: a whole 4x4x8 slice. The times are simulated.
256 devices in a mesh: px: 32 (over z, y), py: 8 (over x, core).
Axes of the slice: x: 4, y: 4, z: 8, core: 2. Of those that a mesh axis runs over, the one named last changes fastest.
Arguments:
- residual: float32 [32, 512, 1024], P(None, 'px', 'py'), may hold values from -6 to 6
- factor_fine: bfloat16 [256, 8, 520, 256], P('px', 'py'), may hold values from -0.25 to 0.25
- factor_one: bfloat16 [128, 4, 520, 256], P('px'), may hold values from -0.25 to 0.25
- factor_two: bfloat16 [64, 2, 520, 256], P('px'), may hold values from -0.25 to 0.25
- factor_three: bfloat16 [32, 1, 520, 256], P('px'), may hold values from -0.25 to 0.25
- factor_four: bfloat16 [16, 1, 264, 128], replicated, may hold values from -0.375 to 0.375
- coarse_inverse: bfloat16 [512, 512], replicated, may hold values from -0.25 to 0.25
Outputs:
- preconditioned: float32 [32, 512, 1024], P(None, 'px', 'py')
All inputs are finite; a program needn't handle non-finite values.
Results may differ from a plain program's by a relative error of at most 0.0029.
Values sent between devices are 32-bit elements; how exact they have to be, the bound alone decides.
A program may use at most 128 MiB of HBM per device.

v0:
```python
import functools

import jax
import jax.numpy as jnp
import numpy as np
from jax import lax
from jax.experimental import pallas as pl
from jax.experimental.pallas import tpu as pltpu
from jax.sharding import PartitionSpec as P

F32 = jnp.float32
BF = jnp.bfloat16
MESH = pl.DeviceIdType.MESH
LANES_FOUR = (6, 16, 38)
ROWS_TWO = ((0, 1, 2), (4, 5, 3))
GROUP_OF = (0, 1, 2, 2, 3, 3, 3, 3, 3)


def composites(count):
    found, now = [], np.eye(count)
    for _ in range(5):
        fine = now.shape[0]
        step = np.zeros((fine // 2, fine))
        for i in range(fine // 2):
            for shift, tap in ((-1, 1), (0, 3), (1, 3), (2, 1)):
                if 0 <= 2 * i + shift < fine:
                    step[i, 2 * i + shift] = tap
        now = step @ now
        found.append(now)
    return found


def pick(matrix, row, low, count):
    if 0 <= row < matrix.shape[0]:
        return matrix[row, low : low + count]
    return np.zeros(count)


def edge_lanes(row):
    slot, first, count = ((0, 0, 2), (1, 2, 3), (3, 5, 3), (2, 8, 2))[(row >= 2) + (row >= 5) + (row >= 8)]
    base = 32 * slot + 18 + 2 * (row - first)
    return base, base + 2 * count


def down_rows(rows, px):
    z, low = px // 4, 16 * px
    a1, a2, a3, a4, a5 = (m / 20.0 ** (i + 1) for i, m in enumerate(rows))
    w = np.zeros((9, 16, 128))
    for s in range(4):
        w[0, :, 32 * s : 32 * s + 6] = pick(a5, 2 * z - 1 + s, low, 16)[:, None]
        w[1, :, 32 * s : 32 * s + 18] = pick(a3, 2 * px - 1 + s, low, 16)[:, None]
    for m, at in enumerate(LANES_FOUR):
        for h in range(2):
            w[0, :, at + 64 * h : at + 64 * h + 10] = pick(a4, 4 * z - 1 + 2 * m + h, low, 16)[:, None]
    for e in range(16):
        w[0, e // 2, 48 + e] = 1.0
        w[0, 8 + e // 2, 112 + e] = 1.0
    for r in range(10):
        for at in edge_lanes(r):
            w[1, :, at : at + 2] = pick(a1, 8 * px - 1 + r, low, 16)[:, None]
    for half in range(2):
        for u in range(3):
            w[2 + half, :, 42 * u : 42 * u + 34] = pick(a2, 4 * px - 1 + ROWS_TWO[half][u], low, 16)[:, None]
    for m in range(5):
        for h in range(2):
            w[4 + m, :, 64 * h : 64 * h + 64] = pick(a1, 8 * px - 1 + 2 * m + h, low, 16)[:, None]
    return w


def down_columns(columns, py):
    b1, b2, b3, b4, b5 = columns
    low = 128 * py
    b = np.zeros((128, 512))
    for s in range(4):
        for c in range(6):
            b[:, 32 * s + c] = pick(b5, 4 * py - 1 + c, low, 128)
        for c in range(18):
            b[:, 128 + 32 * s + c] = pick(b3, 16 * py - 1 + c, low, 128)
    for at in LANES_FOUR:
        for c in range(10):
            b[:, at + c] = b[:, at + 64 + c] = pick(b4, 8 * py - 1 + c, low, 128)
    for e in range(16):
        b[0 if e % 2 else 127, 48 + e] = 1.0
        b[0 if e % 2 else 127, 112 + e] = 1.0
    for r in range(10):
        p, q = edge_lanes(r)
        for at, col in ((p, -1), (p + 1, 0), (q, 63), (q + 1, 64)):
            b[:, 128 + at] = pick(b1, 64 * py + col, low, 128)
    for u in range(3):
        for c in range(34):
            b[:, 256 + 42 * u + c] = pick(b2, 32 * py - 1 + c, low, 128)
    for c in range(64):
        b[:, 384 + c] = b[:, 448 + c] = pick(b1, 64 * py + c, low, 128)
    return b


def up_columns(columns, py):
    b1, b2, b3, b4, b5 = columns
    low, tile, core = 128 * py, 128 * (py // 2), py % 2
    one = np.stack([pick(b1, tile + c, low, 128) for c in range(128)])
    if core == 0:
        one[127] = pick(b1, tile - 1, low, 128)
    else:
        one[0] = pick(b1, tile + 128, low, 128)
    two = np.stack([pick(b2, c, low, 128) for c in range(256)])
    three = np.stack([pick(b3, c, low, 128) for c in range(128)])
    four = np.stack([pick(b4, c % 64, low, 128) for c in range(128)])
    five = np.stack([pick(b5, c % 32, low, 128) for c in range(128)])
    return one, two, three, four, five


def up_rows(rows, px):
    z, low = px // 4, 16 * px
    w = np.zeros((32, 16))
    firsts = ((0, 10, 8 * px - 1), (10, 6, 4 * px - 1), (16, 4, 2 * px - 1), (20, 8, 4 * z - 2), (28, 4, 2 * z - 1))
    for level, (at, count, first) in enumerate(firsts):
        for i in range(count):
            w[at + i] = pick(rows[level], first + i, low, 16) / 20.0 ** (level + 1)
    return w


def split(matrix):
    high = matrix.astype(BF)
    return high, (matrix - high.astype(np.float64)).astype(BF)


@functools.cache
def tables():
    rows, columns = composites(512), composites(1024)
    some = (12, 13, 14, 15, 0, 31)
    down_w = np.stack([down_rows(rows, px) for px in some])
    up_w = np.stack([up_rows(rows, px) for px in some])
    down_b, down_b5 = [], []
    for py in (0, 3, 7):
        high, low = split(down_columns(columns, py))
        down_b.append(high)
        down_b5.append(low[:, :128])
    up = []
    for py in range(8):
        one, two, three, four, five = up_columns(columns, py)
        high, low = split(five)
        up.append(np.concatenate([m.astype(BF) for m in (one, two, three, four)] + [high, low]))
    return (
        down_w.astype(np.float32),
        np.pad(up_w.reshape(6, 4, 128), ((0, 0), (0, 4), (0, 0))).astype(np.float32),
        np.stack(down_b),
        np.stack(down_b5),
        np.stack(up),
    )


def kernel(
    down_used, up_used,
    res_hbm, ff_hbm, f1_hbm, f2_hbm, f3_hbm, f4_hbm, ci_hbm, dw_hbm, uw_hbm, db_hbm, db5_hbm, up_hbm,
    out_ref,
    res, ff, f1, f2, f3, f4, ci, dw, uw, db, db5, up,
    xt, yy, own, sb, pb, xa, xb, xm, yb5, yb4, zb5, f4own, zb4, hs, hb, cs, cb, p0, p5, acc,
    lsem, asend, arecv, bsend, brecv, csend, crecv, msend, mrecv, y5send, y5recv, y4send, y4recv,
    z5send, z5recv, z4send, z4recv, hsend, hrecv, esend, erecv,
):
    px, py = lax.axis_index("px"), lax.axis_index("py")
    z, y = px // 4, px % 4
    x, core = py // 2, py % 2
    has_left, has_right = px > 0, px < 31
    beside = jnp.where(core == 0, py - 1, py + 1)
    has_beside = jnp.logical_and(beside >= 0, beside < 8)
    beside = jnp.clip(beside, 0, 7)
    variant = jnp.where(px == 0, 4, jnp.where(px == 31, 5, y))
    place = jnp.where(py == 0, 0, jnp.where(py == 7, 2, 1))
    lane = lax.broadcasted_iota(jnp.int32, (32, 128), 1)

    def roll(tile, shift):
        if isinstance(shift, int):
            shift %= 128
            return tile if shift == 0 else pltpu.roll(tile, shift, 1)
        return pltpu.roll(tile, shift, 1)

    def only(mask, tile):
        return jnp.where(mask, tile, 0.0)

    local = [
        (res_hbm, res),
        (db_hbm.at[place], db.at[pl.ds(0, 128)]),
        (db_hbm.at[place], db.at[pl.ds(128, 128)]),
        (db5_hbm.at[place], db5),
        (dw_hbm.at[variant], dw),
        (uw_hbm.at[variant], uw),
        (up_hbm.at[py], up),
        (f3_hbm.at[0, 0], f3),
        (f2_hbm, f2),
        (ci_hbm, ci),
        (ff_hbm, ff),
    ]
    local += [(f1_hbm.at[b, x], f1.at[b]) for b in range(4)]
    local += [(f4_hbm.at[jnp.clip(2 * z - 1 + b, 0, 15), 0], f4.at[b]) for b in range(4)]
    local = [pltpu.make_async_copy(s, d, lsem.at[i]) for i, (s, d) in enumerate(local)]
    for copy in local:
        copy.start()

    barrier = pltpu.get_barrier_semaphore()

    def greet(**where):
        pl.semaphore_signal(barrier, inc=1, device_id=where, device_id_type=MESH)

    for d in range(1, 8):
        greet(px=px, py=(py + d) % 8)
        greet(px=((z + d) % 8) * 4 + y, py=py)
    for d in range(1, 4):
        greet(px=z * 4 + (y + d) % 4, py=py)

    @pl.when(has_left)
    def _():
        greet(px=px - 1, py=py)

    @pl.when(has_right)
    def _():
        greet(px=px + 1, py=py)

    @pl.when(jnp.logical_and(has_left, has_beside))
    def _():
        greet(px=px - 1, py=beside)

    @pl.when(jnp.logical_and(has_right, has_beside))
    def _():
        greet(px=px + 1, py=beside)

    def send(src, dst, ssem, rsem, **where):
        return pltpu.make_async_remote_copy(
            src_ref=src, dst_ref=dst, send_sem=ssem, recv_sem=rsem, device_id=where, device_id_type=MESH
        )

    nothing = jnp.zeros((32, 128), F32)

    def clear(ref, *lead):
        ref[lead] = nothing

    for end in (0, 9):
        clear(xa, end)
        clear(zb5, end)
        for i in range(3):
            clear(xb, end, i)

    @pl.when(px == 0)
    def _():
        for i in range(4):
            clear(pb, 0, i)
        for i in range(3):
            clear(hb, 0, i)

    @pl.when(px == 31)
    def _():
        for i in range(4):
            clear(pb, 1, i)
        for i in range(3):
            clear(hb, 1, i)

    @pl.when(z == 0)
    def _():
        for i in range(3):
            clear(zb4, 0, i)

    @pl.when(z == 7)
    def _():
        for i in range(3):
            clear(zb4, 1, i)

    diag = (
        jnp.logical_and(has_beside, has_left),
        has_beside,
        jnp.logical_and(has_beside, has_right),
    )
    for i in range(3):

        @pl.when(jnp.logical_not(diag[i]))
        def _(i=i):
            clear(cb, i)

    local[0].wait()
    for f in range(16):
        xt[f] = res[pl.ds(f, 32, stride=16), :]
    rows = xt[...].reshape(512, 128)
    high = rows.astype(BF)
    low = (rows - high.astype(F32)).astype(BF)
    both = jnp.concatenate([high, low], axis=1)
    for i in range(1, 5):
        local[i].wait()
    yy[:, :256] = jnp.dot(both, db[:, :256], preferred_element_type=F32)
    yy[:, :128] += jnp.dot(high, db5[...], preferred_element_type=F32)

    def packed(t):
        at = 128 * GROUP_OF[t]
        total = None
        for f in range(16):
            if down_used[t][f]:
                term = yy[32 * f : 32 * f + 32, at : at + 128] * dw[t, f : f + 1, :]
                total = term if total is None else total + term
        return total

    xa[py + 1] = packed(0)
    pl.semaphore_wait(
        barrier,
        17 + jnp.where(has_left, 1, 0) + jnp.where(has_right, 1, 0) + jnp.where(diag[0], 1, 0) + jnp.where(diag[2], 1, 0),
    )

    def to_py(buffer, ssem, rsem, d, slot):
        return send(buffer.at[slot + 1], buffer.at[slot + 1], ssem.at[d - 1], rsem.at[slot], px=px, py=(py + d) % 8)

    sent = []
    for d in (4, 3, 5, 2, 6, 1, 7):
        copy = to_py(xa, asend, arecv, d, py)
        copy.start()
        sent.append(copy)

    yy[:, 256:] = jnp.dot(both, db[:, 256:], preferred_element_type=F32)
    for t in range(1, 9):
        own[t - 1] = packed(t)
    sb[0, 0] = own[0]
    sb[1, 0] = own[0]
    sb[0, 1] = own[1]
    sb[1, 1] = own[2]
    sb[0, 2] = own[3]
    sb[1, 2] = own[7]
    sb[0, 3] = xt[0]
    sb[1, 3] = xt[15]

    def to_left(src, dst, ssem, rsem):
        return send(src.at[0], dst.at[1], ssem.at[0], rsem.at[1], px=px - 1, py=py)

    def to_right(src, dst, ssem, rsem):
        return send(src.at[1], dst.at[0], ssem.at[1], rsem.at[0], px=px + 1, py=py)

    def start_rows(*refs):
        @pl.when(has_left)
        def _():
            to_left(*refs).start()

        @pl.when(has_right)
        def _():
            to_right(*refs).start()

    def got_rows(src, dst, ssem, rsem):
        @pl.when(has_left)
        def _():
            send(src.at[1], dst.at[0], ssem.at[1], rsem.at[0], px=px - 1, py=py).wait_recv()

        @pl.when(has_right)
        def _():
            send(src.at[0], dst.at[1], ssem.at[0], rsem.at[1], px=px + 1, py=py).wait_recv()

    def sent_rows(*refs):
        @pl.when(has_left)
        def _():
            to_left(*refs).wait_send()

        @pl.when(has_right)
        def _():
            to_right(*refs).wait_send()

    start_rows(sb, pb, bsend, brecv)

    for d in range(1, 8):
        to_py(xa, asend, arecv, d, (py + 8 - d) % 8).wait_recv()
    five = None
    fours = [None] * 3
    for p in range(8):
        tile = xa[p + 1]
        term = only(((lane - 4 * p + 1) & 31) < 6, roll(tile, 4 * p - 1))
        five = term if five is None else five + term
        near = ((lane - 8 * p + 1) & 63) < 10
        for m in range(3):
            term = only(near, roll(tile, 8 * p - 1 - LANES_FOUR[m]))
            fours[m] = term if fours[m] is None else fours[m] + term
    yb5[y] = five
    for m in range(3):
        yb4[y, m] = fours[m]

    def to_y(buffer, ssem, rsem, d, slot):
        return send(buffer.at[slot], buffer.at[slot], ssem.at[d - 1], rsem.at[slot], px=z * 4 + (y + d) % 4, py=py)

    for d in (2, 1, 3):
        copy = to_y(yb5, y5send, y5recv, d, y)
        copy.start()
        sent.append(copy)
    for d in (2, 1, 3):
        copy = to_y(yb4, y4send, y4recv, d, y)
        copy.start()
        sent.append(copy)

    got_rows(sb, pb, bsend, brecv)
    mine = own[0]
    across = jnp.where(lane < 64, roll(pb[0, 0], 64), roll(pb[1, 0], 64))
    inside = jnp.logical_or((lane & 63) < 50, (lane & 63) > 61)
    mine = mine + only(inside, across)
    corner = jnp.where(lane < 28, roll(pb[0, 3], 27), roll(pb[1, 3], 29))
    mine = jnp.where(jnp.logical_and(lane >= 26, lane < 30), corner, mine)
    xb[py + 1, 0] = mine
    xb[py + 1, 1] = own[1] + only(lane < 84, pb[0, 1])
    xb[py + 1, 2] = own[2] + only(lane < 84, pb[1, 1])
    xm[core, 0] = own[3] + pb[0, 2]
    for m in range(1, 4):
        xm[core, m] = own[3 + m]
    xm[core, 4] = own[7] + pb[1, 2]

    def to_partner(slot):
        return send(xm.at[slot], xm.at[slot], msend, mrecv, px=px, py=2 * x + 1 - core)

    to_partner(core).start()
    sent.append(to_partner(core))
    for d in (4, 3, 5, 2, 6, 1, 7):
        copy = to_py(xb, csend, crecv, d, py)
        copy.start()
        sent.append(copy)

    for d in range(1, 4):
        to_y(yb5, y5send, y5recv, d, (y + 4 - d) % 4).wait_recv()
    zb5[z + 1] = (yb5[0] + yb5[1]) + (yb5[2] + yb5[3])

    def to_z(d, slot):
        return send(zb5.at[slot + 1], zb5.at[slot + 1], z5send.at[d - 1], z5recv.at[slot], px=((z + d) % 8) * 4 + y, py=py)

    for d in (4, 3, 5, 2, 6, 1, 7):
        copy = to_z(d, z)
        copy.start()
        sent.append(copy)
    for d in range(1, 4):
        to_y(yb4, y4send, y4recv, d, (y + 4 - d) % 4).wait_recv()
    for m in range(3):
        f4own[m] = (yb4[0, m] + yb4[1, m]) + (yb4[2, m] + yb4[3, m])

    def z4_down():
        return send(f4own, zb4.at[1], z4send.at[0], z4recv.at[1], px=px - 4, py=py)

    def z4_up():
        return send(f4own, zb4.at[0], z4send.at[1], z4recv.at[0], px=px + 4, py=py)

    @pl.when(z > 0)
    def _():
        z4_down().start()

    @pl.when(z < 7)
    def _():
        z4_up().start()

    def solve(windows, factor):
        return jnp.dot(windows.astype(BF), factor, preferred_element_type=F32)

    def window(shifted, halo):
        parts = [jnp.where(lane == 0, halo(0), shifted[0])]
        for j in range(1, 4):
            parts.append(jnp.where(lane <= 2 * j - 2, shifted[j - 1], jnp.where(lane <= 2 * j, halo(j), shifted[j])))
        last = jnp.where(lane <= 6, shifted[3], halo(4))
        return jnp.concatenate(parts + [last[:, :8]], axis=1)

    def lifted(tiles, table):
        count = 32 * len(tiles)
        fine = jnp.concatenate(tiles, axis=0)
        top = fine.astype(BF)
        rest = (fine - top.astype(F32)).astype(BF)
        product = jnp.dot(jnp.concatenate([top, rest], axis=0), table, preferred_element_type=F32)
        product = product[:count] + product[count:]
        return [product[32 * i : 32 * i + 32] for i in range(len(tiles))]

    for d in range(1, 8):
        to_py(xb, csend, crecv, d, (py + 8 - d) % 8).wait_recv()
    local[6].wait()
    local[7].wait()
    rows_three = []
    for s in range(4):
        total = None
        for p in range(8):
            near = jnp.logical_and(lane >= 16 * p - 1, lane <= 16 * p + 16)
            term = only(near, roll(xb[p + 1, 0], 16 * p - 1 - 32 * s))
            total = term if total is None else total + term
        rows_three.append(total)
    shifted = [roll(rows_three[k], 2 * k + 1) for k in range(4)]
    solved = solve(window(shifted, lambda j: nothing), f3[...])
    three = lifted([solved[:, :128], solved[:, 128:]], up[384:512, :])
    hs[0, 2] = three[0]
    hs[1, 2] = three[1]

    rows_two = []
    for r in range(6):
        half, u = next((h, ROWS_TWO[h].index(r)) for h in range(2) if r in ROWS_TWO[h])
        pair = [None, None]
        for p in range(8):
            turned = roll(xb[p + 1, 1 + half], 32 * p - 1 - 42 * u)
            first = 32 * (p % 4) - 1
            near = jnp.logical_and(lane >= first, lane <= first + 33)
            term = only(near, turned)
            pair[p // 4] = term if pair[p // 4] is None else pair[p // 4] + term
            if p == 3:
                pair[1] = only(lane == 0, turned)
            if p == 4:
                pair[0] = pair[0] + only(lane == 127, turned)
        rows_two.append(pair)
    local[8].wait()
    two = []
    for b in range(2):
        turned = [[roll(rows_two[2 * b + k][t], 2 * k + 1) for k in range(4)] for t in range(2)]

        def right_of(j, turned=turned):
            return only(lane == 2 * j - 1, turned[1][j - 1]) if j > 0 else nothing

        def left_of(j, turned=turned):
            return only(lane == 2 * j, turned[0][j]) if j < 4 else nothing

        left_tile = solve(window(turned[0], right_of), f2[b, 0])
        right_tile = solve(window(turned[1], left_of), f2[b, 1])
        for h in range(2):
            at = slice(128 * h, 128 * h + 128)
            two.append((left_tile[:, at], right_tile[:, at]))
    part = lifted([pair[0] for pair in two], up[128:256, :])
    other = lifted([pair[1] for pair in two], up[256:384, :])
    two = [a + b for a, b in zip(part, other)]
    hs[0, 1] = two[0]
    hs[1, 1] = two[3]

    to_partner(1 - core).wait_recv()
    left_edge, first_edge, second_edge, right_edge = (xb[2 * x + i, 0] for i in range(4))
    even = (lane & 1) == 0

    def edges(n):
        mid = jnp.where(even, second_edge, roll(first_edge, -n))
        outer = jnp.where(even, right_edge, roll(left_edge, -n))
        halo = jnp.where(even, first_edge + roll(left_edge, -n), right_edge + roll(second_edge, -n))
        return mid, outer, halo

    edges_of = {2: edges(4), 3: edges(6)}
    rows_one = []
    for r in range(10):
        m, h = divmod(r, 2)
        if h == 0:
            main = jnp.where(lane < 64, xm[0, m], roll(xm[1, m], 64))
        else:
            main = jnp.where(lane < 64, roll(xm[0, m], 64), xm[1, m])
        at, last = edge_lanes(r)
        mid, outer, _ = edges_of[(last - at) // 2]
        main = main + only(jnp.logical_or(lane == 63, lane == 64), roll(mid, 63 - at))
        main = main + only(jnp.logical_or(lane == 127, lane == 0), roll(outer, 127 - at))
        rows_one.append(main)
    halo_two, halo_three = edges_of[2][2], edges_of[3][2]
    halos = jnp.where(
        lane < 4,
        roll(halo_two, -18),
        jnp.where(lane < 10, roll(halo_three, -46), jnp.where(lane < 16, roll(halo_three, -104), roll(halo_two, -66))),
    )
    one = []
    for b in range(4):
        local[11 + b].wait()
        turned = [roll(rows_one[2 * b + k], 2 * k + 1) for k in range(4)]
        side = roll(halos, -4 * b)
        solved = solve(window(turned, lambda j, side=side: side), f1[b])
        one += [solved[:, :128], solved[:, 128:]]
    hs[0, 0] = one[0]
    hs[1, 0] = one[7]
    start_rows(hs, hb, hsend, hrecv)
    column = nothing
    for r in range(8):
        column = jnp.where(lane == r, roll(one[r], r + core), column)
    cs[...] = column

    def to_side(d):
        return send(cs, cb.at[1 - d], esend.at[1 - d], erecv.at[1 - d], px=px + d, py=beside)

    for d in (-1, 1, 0):

        @pl.when(diag[1 + d])
        def _(d=d):
            to_side(d).start()

    before, after = xa[py], xa[py + 2]
    corner_before, corner_after = xb[py, 0], xb[py + 2, 0]
    facing = jnp.where(even, before, after)
    corners = jnp.where(even, corner_before, corner_after)
    halos = jnp.where(
        lane < 2,
        roll(corners, -26),
        jnp.where(lane < 18, roll(facing, -46), jnp.where(lane < 34, roll(facing, -94), roll(corners, 6))),
    )
    local[10].wait()
    for b in range(8):
        tiles = []
        for k in range(4):
            at = 2 * b + k
            tile = pb[0, 3] if at == 0 else pb[1, 3] if at == 17 else xt[at - 1]
            tiles.append(roll(tile, 2 * k + 1))
        side = roll(halos, -4 * b)
        solved = solve(window(tiles, lambda j, side=side: side), ff[b, 0])
        p0[2 * b] = solved[:, :128]
        p0[2 * b + 1] = solved[:, 128:]

    @pl.when(z > 0)
    def _():
        send(f4own, zb4.at[0], z4send.at[1], z4recv.at[0], px=px - 4, py=py).wait_recv()

    @pl.when(z < 7)
    def _():
        send(f4own, zb4.at[1], z4send.at[0], z4recv.at[1], px=px + 4, py=py).wait_recv()

    quads = (zb4[0, 1], zb4[0, 2] + f4own[0], f4own[1], f4own[2] + zb4[1, 0], zb4[1, 1])
    fours = []
    for b in range(4):
        local[15 + b].wait()
        first, second = quads[b], quads[b + 1]
        v0 = jnp.where(
            lane <= 64,
            only(lane >= 1, roll(first, 1)),
            only(lane >= 67, roll(first, 3)),
        )
        v1 = jnp.where(
            lane <= 2,
            roll(first, 3),
            jnp.where(lane <= 68, only(lane >= 5, roll(second, 5)), only(lane >= 71, roll(second, 7))),
        )
        v2 = only(lane <= 6, roll(second, 7))
        solved = solve(jnp.concatenate([v0, v1, v2[:, :8]], axis=1), f4[b])
        fours += [only(lane < 64, solved), only(lane >= 64, solved)]
    four = lifted(fours, up[512:640, :])

    got_rows(hs, hb, hsend, hrecv)
    for d in (-1, 0, 1):

        @pl.when(diag[1 + d])
        def _(d=d):
            send(cs, cb.at[1 + d], esend.at[1 + d], erecv.at[1 + d], px=px + d, py=beside).wait_recv()

    one = [hb[0, 0]] + one + [hb[1, 0]]
    at_lane = 127 * (1 - core)
    for r in range(10):
        source, from_lane = (0, 7) if r == 0 else (2, 0) if r == 9 else (1, r - 1)
        one[r] = jnp.where(lane == at_lane, roll(cb[source], (at_lane - from_lane + 128) % 128), one[r])
    one = lifted(one, up[0:128, :])
    two = [hb[0, 1]] + two + [hb[1, 1]]
    three = [hb[0, 2]] + three + [hb[1, 2]]
    local[5].wait()
    terms = one + two + three + four
    for f in range(16):
        total = p0[f]
        for r in range(28):
            if up_used[r][f]:
                total = total + uw[r // 8, 16 * (r % 8) + f] * terms[r]
        acc[f] = total

    for d in range(1, 8):
        to_z(d, (z + 8 - d) % 8).wait_recv()
    local[9].wait()
    down = [roll(zb5[i + 1], -32) if i < 8 else nothing for i in range(0, 10, 2)]
    rise = [nothing] + [roll(zb5[i + 1], 32) for i in range(1, 8, 2)]
    flat = [
        jnp.where(lane < 96, down[j], down[j + 1]) + jnp.where(lane >= 32, rise[j + 1], rise[j]) for j in range(4)
    ]
    solved = solve(jnp.concatenate(flat, axis=1), ci[...])
    clear(p5, 0)
    clear(p5, 5)
    for j in range(4):
        p5[j + 1] = solved[:, 128 * j : 128 * j + 128]
    odd = z % 2
    lead = (z + odd) // 2
    edge = 32 + 64 * odd
    five = jnp.where(lane < edge, roll(p5[lead], edge), roll(p5[lead + 1], edge))
    fives = [only((lane // 32) == s, five) for s in range(4)]
    full = jnp.concatenate(fives, axis=0)
    top = full.astype(BF)
    rest = (full - top.astype(F32)).astype(BF)
    product = jnp.dot(jnp.concatenate([top, rest], axis=0), up[640:768, :], preferred_element_type=F32)
    product = product[:128] + product[128:] + jnp.dot(top, up[768:896, :], preferred_element_type=F32)
    for f in range(16):
        total = acc[f]
        for s in range(4):
            if up_used[28 + s][f]:
                total = total + uw[3, 16 * (4 + s) + f] * product[32 * s : 32 * s + 32]
        out_ref[pl.ds(f, 32, stride=16), :] = total

    for copy in sent:
        copy.wait_send()
    sent_rows(sb, pb, bsend, brecv)
    sent_rows(hs, hb, hsend, hrecv)

    @pl.when(z > 0)
    def _():
        z4_down().wait_send()

    @pl.when(z < 7)
    def _():
        z4_up().wait_send()

    for d in (-1, 0, 1):

        @pl.when(diag[1 + d])
        def _(d=d):
            to_side(d).wait_send()


def per_device(residual, fine, one, two, three, four, inverse):
    down_w, up_w, down_b, down_b5, up = tables()
    down_used = (down_w != 0).any(axis=(0, 3)).tolist()
    up_used = (up_w[:, :4] != 0).any(axis=0).reshape(32, 16).tolist()
    tile = (32, 128)

    def tiles(*lead):
        return pltpu.VMEM(lead + tile, F32)

    dma = pltpu.SemaphoreType.DMA
    out = pl.pallas_call(
        functools.partial(kernel, down_used, up_used),
        out_shape=jax.ShapeDtypeStruct((512, 128), F32),
        in_specs=[pl.BlockSpec(memory_space=pltpu.HBM)] * 12,
        out_specs=pl.BlockSpec(memory_space=pltpu.VMEM),
        scratch_shapes=[
            pltpu.VMEM((512, 128), F32),
            pltpu.VMEM((8, 1, 520, 256), BF),
            pltpu.VMEM((4, 520, 256), BF),
            pltpu.VMEM((2, 2, 520, 256), BF),
            pltpu.VMEM((520, 256), BF),
            pltpu.VMEM((4, 264, 128), BF),
            pltpu.VMEM((512, 512), BF),
            pltpu.VMEM((9, 16, 128), F32),
            pltpu.SMEM((8, 128), F32),
            pltpu.VMEM((256, 512), BF),
            pltpu.VMEM((128, 128), BF),
            pltpu.VMEM((896, 128), BF),
            tiles(16),
            pltpu.VMEM((512, 512), F32),
            tiles(8),
            tiles(2, 4),
            tiles(2, 4),
            tiles(10),
            tiles(10, 3),
            tiles(2, 5),
            tiles(4),
            tiles(4, 3),
            tiles(10),
            tiles(3),
            tiles(2, 3),
            tiles(2, 3),
            tiles(2, 3),
            tiles(),
            tiles(3),
            tiles(16),
            tiles(6),
            tiles(16),
            dma((19,)),
            dma((7,)),
            dma((8,)),
            dma((2,)),
            dma((2,)),
            dma((7,)),
            dma((8,)),
            dma,
            dma,
            dma((3,)),
            dma((4,)),
            dma((3,)),
            dma((4,)),
            dma((7,)),
            dma((8,)),
            dma((2,)),
            dma((2,)),
            dma((2,)),
            dma((2,)),
            dma((3,)),
            dma((3,)),
        ],
        compiler_params=pltpu.CompilerParams(collective_id=0, has_side_effects=True, vmem_limit_bytes=48 << 20),
    )(
        residual.reshape(512, 128), fine, one, two, three, four, inverse,
        jnp.asarray(down_w), jnp.asarray(up_w), jnp.asarray(down_b), jnp.asarray(down_b5), jnp.asarray(up),
    )
    return out.reshape(32, 16, 128)


def solution(mesh):
    placed = (
        P(None, "px", "py"),
        P("px", "py", None, None),
        P("px", None, None, None),
        P("px", None, None, None),
        P("px", None, None, None),
        P(),
        P(),
    )
    return jax.shard_map(
        per_device, mesh=mesh, in_specs=placed, out_specs=P(None, "px", "py"), check_vma=False
    )
```

profile of v0, /device:TPU:33, one launch (start us, length us, event | category | flops | bytes accessed | tf_op | source)
XLA Modules:
  0.0 39.0 jit_solution(13595200022738195313)
XLA Ops:
  0.0 0.0 copy-start
  0.0 1.2 %copy-done = bf16[16,1,264,128]{3,2,1,0:T(8,128)(2,1)S(1)} copy-done((bf16[16,1,264,128]{3,2,1,0:T(8,128)(2,1)S(1)}, bf16[16,1,264,128]{3,2,1,0:T(8,128)(2,1)}, u32[]{:S(2)}) %copy-start) | copy-done | bytes 1081368
  1.2 0.0 copy-start.1
  1.2 1.2 %copy-done.1 = bf16[2,2,520,256]{3,2,1,0:T(8,128)(2,1)S(1)} copy-done((bf16[2,2,520,256]{3,2,1,0:T(8,128)(2,1)S(1)}, bf16[2,2,520,256]{3,2,1,0:T(8,128)(2,1)}, u32[]{:S(2)}) %copy-start.1) | copy-done | bytes 1064984
  2.5 0.0 copy-start.2
  2.5 1.0 %copy-done.2 = bf16[512,512]{1,0:T(8,128)(2,1)S(1)} copy-done((bf16[512,512]{1,0:T(8,128)(2,1)S(1)}, bf16[512,512]{1,0:T(8,128)(2,1)}, u32[]{:S(2)}) %copy-start.2) | copy-done | bytes 524312
  3.5 0.0 copy-start.3
  3.5 1.0 %copy-done.3 = f32[6,9,16,128]{3,2,1,0:T(8,128)S(1)} copy-done((f32[6,9,16,128]{3,2,1,0:T(8,128)S(1)}, f32[6,9,16,128]{3,2,1,0:T(8,128)}, u32[]{:S(2)}) %copy-start.3) | copy-done | bytes 442392
  4.5 0.0 copy-start.4
  4.5 1.0 %copy-done.4 = bf16[3,128,512]{2,1,0:T(8,128)(2,1)S(1)} copy-done((bf16[3,128,512]{2,1,0:T(8,128)(2,1)S(1)}, bf16[3,128,512]{2,1,0:T(8,128)(2,1)}, u32[]{:S(2)}) %copy-start.4) | copy-done | bytes 393240
  5.5 0.0 copy-start.5
  5.5 0.9 %copy-done.5 = bf16[1,1,520,256]{3,2,1,0:T(8,128)(2,1)S(1)} copy-done((bf16[1,1,520,256]{3,2,1,0:T(8,128)(2,1)S(1)}, bf16[1,1,520,256]{3,2,1,0:T(8,128)(2,1)}, u32[]{:S(2)}) %copy-start.5) | copy-done | bytes 266264
  6.5 0.0 copy-start.6
  6.5 0.9 %copy-done.6 = f32[32,16,128]{2,1,0:T(8,128)S(1)} copy-done((f32[32,16,128]{2,1,0:T(8,128)S(1)}, f32[32,16,128]{2,1,0:T(8,128)}, u32[]{:S(2)}) %copy-start.6) | copy-done | bytes 262168
  7.4 0.0 copy-start.7
  7.4 0.9 %copy-done.7 = bf16[3,128,128]{2,1,0:T(8,128)(2,1)S(1)} copy-done((bf16[3,128,128]{2,1,0:T(8,128)(2,1)S(1)}, bf16[3,128,128]{2,1,0:T(8,128)(2,1)}, u32[]{:S(2)}) %copy-start.7) | copy-done | bytes 98328
  8.3 0.0 copy-start.8
  8.3 0.7 %copy-done.8 = f32[6,8,128]{2,1,0:T(8,128)S(1)} copy-done((f32[6,8,128]{2,1,0:T(8,128)S(1)}, f32[6,8,128]{2,1,0:T(8,128)}, u32[]{:S(2)}) %copy-start.8) | copy-done | bytes 24600
  9.1 29.2 %shard_map.118 = f32[512,128]{1,0:T(8,128)S(1)} custom-call(f32[512,128]{1,0:T(8,128)S(1)} %bitcast.3, bf16[8,1,520,256]{3,2,1,0:T(8,128)(2,1)} %ff_hbm.1, bf16[4,4,520,256]{3,2,1,0:T(8,128)(2,1)} %f1_hbm.1, bf16[2,2,520,256]{3,2,1,0:T(8,128)(2,1)S(1)} %copy-done.1, bf16[1,1,520,256]{3,2,1,0:T(8,128)(2,1)S(1)} %copy-done.5, ...), custom_call_target="tpu_custom_call" | custom-call | tf_op jit(solution)/shard_map/pallas_call | solution.py:704
  38.3 0.7 %copy.14 = f32[32,16,128]{2,1,0:T(8,128)} copy(f32[32,16,128]{2,1,0:T(8,128)S(1)} %bitcast.2) | data formatting | bytes 524288
Async XLA Ops:
  0.0 1.2 %copy-start = (bf16[16,1,264,128]{3,2,1,0:T(8,128)(2,1)S(1)}, bf16[16,1,264,128]{3,2,1,0:T(8,128)(2,1)}, u32[]{:S(2)}) copy-start(bf16[16,1,264,128]{3,2,1,0:T(8,128)(2,1)} %f4_hbm.1) | copy-start | bytes 3244036
  1.2 1.2 %copy-start.1 = (bf16[2,2,520,256]{3,2,1,0:T(8,128)(2,1)S(1)}, bf16[2,2,520,256]{3,2,1,0:T(8,128)(2,1)}, u32[]{:S(2)}) copy-start(bf16[2,2,520,256]{3,2,1,0:T(8,128)(2,1)} %f2_hbm.1) | copy-start | bytes 3194884
  2.5 1.0 %copy-start.2 = (bf16[512,512]{1,0:T(8,128)(2,1)S(1)}, bf16[512,512]{1,0:T(8,128)(2,1)}, u32[]{:S(2)}) copy-start(bf16[512,512]{1,0:T(8,128)(2,1)} %ci_hbm.1) | copy-start | bytes 1572868
  3.5 1.0 %copy-start.3 = (f32[6,9,16,128]{3,2,1,0:T(8,128)S(1)}, f32[6,9,16,128]{3,2,1,0:T(8,128)}, u32[]{:S(2)}) copy-start(f32[6,9,16,128]{3,2,1,0:T(8,128)} %constant.10.clone.dw_hbm) | copy-start | bytes 1327108
  4.5 1.0 %copy-start.4 = (bf16[3,128,512]{2,1,0:T(8,128)(2,1)S(1)}, bf16[3,128,512]{2,1,0:T(8,128)(2,1)}, u32[]{:S(2)}) copy-start(bf16[3,128,512]{2,1,0:T(8,128)(2,1)} %constant.12.clone.db_hbm) | copy-start | bytes 1179652
  5.5 1.0 %copy-start.5 = (bf16[1,1,520,256]{3,2,1,0:T(8,128)(2,1)S(1)}, bf16[1,1,520,256]{3,2,1,0:T(8,128)(2,1)}, u32[]{:S(2)}) copy-start(bf16[1,1,520,256]{3,2,1,0:T(8,128)(2,1)} %f3_hbm.1) | copy-start | bytes 798724
  6.5 0.9 %copy-start.6 = (f32[32,16,128]{2,1,0:T(8,128)S(1)}, f32[32,16,128]{2,1,0:T(8,128)}, u32[]{:S(2)}) copy-start(f32[32,16,128]{2,1,0:T(8,128)} %param.12) | copy-start | bytes 786436
  7.4 0.9 %copy-start.7 = (bf16[3,128,128]{2,1,0:T(8,128)(2,1)S(1)}, bf16[3,128,128]{2,1,0:T(8,128)(2,1)}, u32[]{:S(2)}) copy-start(bf16[3,128,128]{2,1,0:T(8,128)(2,1)} %constant.13.clone.db5_hbm) | copy-start | bytes 294916
  8.3 0.7 %copy-start.8 = (f32[6,8,128]{2,1,0:T(8,128)S(1)}, f32[6,8,128]{2,1,0:T(8,128)}, u32[]{:S(2)}) copy-start(f32[6,8,128]{2,1,0:T(8,128)} %constant.11.clone.uw_hbm) | copy-start | bytes 73732
where the time goes:
time: 39.4 us; the launch traced here: 39 us
  Pallas kernels  29.2 us (74%)
  local copies, waits for them, and re-layouts  9.75 us (25%)
    pallas_call x1, Pallas kernels, per_device(): pl.pallas_call(functools.partial(kernel, down_used, up_used), out_shape=j...  29.2 us
    unnamed x19, local copies, waits for them, and re-layouts  9.75 us

commit v1 on v0

--- a/solution.py
+++ b/solution.py
@@ -761,7 +761,7 @@
             dma((3,)),
             dma((3,)),
         ],
-        compiler_params=pltpu.CompilerParams(collective_id=0, has_side_effects=True, vmem_limit_bytes=48 << 20),
+        compiler_params=pltpu.CompilerParams(collective_id=0, has_side_effects=True, vmem_limit_bytes=67043328),
     )(
         residual.reshape(512, 128), fine, one, two, three, four, inverse,
         jnp.asarray(down_w), jnp.asarray(up_w), jnp.asarray(down_b), jnp.asarray(down_b5), jnp.asarray(up),

time: 39.4 us -> 30.7 us (0.78)
  the two profiles are of different devices: /device:TPU:33 before, /device:TPU:32 now
where the time goes in v1:
time: 30.7 us; the launch traced here: 30.1 us
  Pallas kernels  28.4 us (93%)
  local copies, waits for them, and re-layouts  1.67 us (5%)
    pallas_call x1, Pallas kernels, per_device(): pl.pallas_call(functools.partial(kernel, down_used, up_used), out_shape=j...  28.4 us
    unnamed x1, local copies, waits for them, and re-layouts  1.67 us

profile of v1, /device:TPU:32, one launch (start us, length us, event | category | flops | bytes accessed | tf_op | source)
XLA Modules:
  0.0 30.1 jit_solution(12867292667048842655)
XLA Ops:
  0.0 28.4 %shard_map.118 = f32[512,128]{1,0:T(8,128)} custom-call(f32[512,128]{1,0:T(8,128)} %bitcast.3, bf16[8,1,520,256]{3,2,1,0:T(8,128)(2,1)} %ff_hbm.1, bf16[4,4,520,256]{3,2,1,0:T(8,128)(2,1)} %f1_hbm.1, bf16[2,2,520,256]{3,2,1,0:T(8,128)(2,1)} %f2_hbm.1, bf16[1,1,520,256]{3,2,1,0:T(8,128)(2,1)} %f3_hbm.1, bf16[16,1,264,128]{3,2,1,0:T(8,128)(2,1)} %f4_hbm.1, ...), custom_call_target="tpu_custom_call" | custom-call | tf_op jit(solution)/shard_map/pallas_call | solution.py:704
  28.4 1.7 %copy.14 = f32[32,16,128]{2,1,0:T(8,128)} copy(f32[32,16,128]{2,1,0:T(8,128)} %bitcast.2) | data formatting | bytes 524288

commit v2 on v1

v2 whole, which is shorter than its diff:
```python
import functools

import jax
import jax.numpy as jnp
import numpy as np
from jax import lax
from jax.experimental import pallas as pl
from jax.experimental.pallas import tpu as pltpu
from jax.sharding import PartitionSpec as P

F32 = jnp.float32
BF = jnp.bfloat16
MESH = pl.DeviceIdType.MESH
LANES_FOUR = (6, 16, 38)
ROWS_TWO = ((0, 1, 2), (4, 5, 3))
GROUP_OF = (0, 1, 2, 2, 3, 3, 3, 3, 3)


def composites(count):
    found, now = [], np.eye(count)
    for _ in range(5):
        fine = now.shape[0]
        step = np.zeros((fine // 2, fine))
        for i in range(fine // 2):
            for shift, tap in ((-1, 1), (0, 3), (1, 3), (2, 1)):
                if 0 <= 2 * i + shift < fine:
                    step[i, 2 * i + shift] = tap
        now = step @ now
        found.append(now)
    return found


def pick(matrix, row, low, count):
    if 0 <= row < matrix.shape[0]:
        return matrix[row, low : low + count]
    return np.zeros(count)


def edge_lanes(row):
    slot, first, count = ((0, 0, 2), (1, 2, 3), (3, 5, 3), (2, 8, 2))[(row >= 2) + (row >= 5) + (row >= 8)]
    base = 32 * slot + 18 + 2 * (row - first)
    return base, base + 2 * count


def down_rows(rows, px):
    z, low = px // 4, 16 * px
    a1, a2, a3, a4, a5 = (m / 20.0 ** (i + 1) for i, m in enumerate(rows))
    w = np.zeros((9, 16, 128))
    for s in range(4):
        w[0, :, 32 * s : 32 * s + 6] = pick(a5, 2 * z - 1 + s, low, 16)[:, None]
        w[1, :, 32 * s : 32 * s + 18] = pick(a3, 2 * px - 1 + s, low, 16)[:, None]
    for m, at in enumerate(LANES_FOUR):
        for h in range(2):
            w[0, :, at + 64 * h : at + 64 * h + 10] = pick(a4, 4 * z - 1 + 2 * m + h, low, 16)[:, None]
    for e in range(16):
        w[0, e // 2, 48 + e] = 1.0
        w[0, 8 + e // 2, 112 + e] = 1.0
    for r in range(10):
        for at in edge_lanes(r):
            w[1, :, at : at + 2] = pick(a1, 8 * px - 1 + r, low, 16)[:, None]
    for half in range(2):
        for u in range(3):
            w[2 + half, :, 42 * u : 42 * u + 34] = pick(a2, 4 * px - 1 + ROWS_TWO[half][u], low, 16)[:, None]
    for m in range(5):
        for h in range(2):
            w[4 + m, :, 64 * h : 64 * h + 64] = pick(a1, 8 * px - 1 + 2 * m + h, low, 16)[:, None]
    return w


def down_columns(columns, py):
    b1, b2, b3, b4, b5 = columns
    low = 128 * py
    b = np.zeros((128, 512))
    for s in range(4):
        for c in range(6):
            b[:, 32 * s + c] = pick(b5, 4 * py - 1 + c, low, 128)
        for c in range(18):
            b[:, 128 + 32 * s + c] = pick(b3, 16 * py - 1 + c, low, 128)
    for at in LANES_FOUR:
        for c in range(10):
            b[:, at + c] = b[:, at + 64 + c] = pick(b4, 8 * py - 1 + c, low, 128)
    for e in range(16):
        b[0 if e % 2 else 127, 48 + e] = 1.0
        b[0 if e % 2 else 127, 112 + e] = 1.0
    for r in range(10):
        p, q = edge_lanes(r)
        for at, col in ((p, -1), (p + 1, 0), (q, 63), (q + 1, 64)):
            b[:, 128 + at] = pick(b1, 64 * py + col, low, 128)
    for u in range(3):
        for c in range(34):
            b[:, 256 + 42 * u + c] = pick(b2, 32 * py - 1 + c, low, 128)
    for c in range(64):
        b[:, 384 + c] = b[:, 448 + c] = pick(b1, 64 * py + c, low, 128)
    return b


def up_one(columns, py):
    low, tile = 128 * py, 128 * (py // 2)
    one = np.stack([pick(columns[0], tile + c, low, 128) for c in range(128)])
    if py % 2 == 0:
        one[127] = pick(columns[0], tile - 1, low, 128)
    else:
        one[0] = pick(columns[0], tile + 128, low, 128)
    return one, np.stack([pick(columns[4], c % 32, low, 128) for c in range(128)])


def up_near(columns, py):
    low = 128 * py
    two, three, four = (np.zeros((128, 128)) for _ in range(3))
    for u in range(3):
        for c in range(34):
            two[42 * u + c] = pick(columns[1], 32 * py - 1 + c, low, 128)
    for s in range(4):
        for c in range(18):
            three[32 * s + c] = pick(columns[2], 16 * py - 1 + c, low, 128)
        for c in range(10):
            four[10 * s + c] = four[64 + 10 * s + c] = pick(columns[3], 8 * py - 1 + c, low, 128)
    return np.concatenate([two, three, four])


def up_rows(rows, px):
    z, low = px // 4, 16 * px
    w = np.zeros((32, 16))
    firsts = ((0, 10, 8 * px - 1), (10, 6, 4 * px - 1), (16, 4, 2 * px - 1), (20, 8, 4 * z - 2), (28, 4, 2 * z - 1))
    for level, (at, count, first) in enumerate(firsts):
        for i in range(count):
            w[at + i] = pick(rows[level], first + i, low, 16) / 20.0 ** (level + 1)
    return w


def split(matrix):
    high = matrix.astype(BF)
    return high, (matrix - high.astype(np.float64)).astype(BF)


@functools.cache
def tables():
    rows, columns = composites(512), composites(1024)
    some = (12, 13, 14, 15, 0, 31)
    down_w = np.stack([down_rows(rows, px) for px in some])
    up_w = np.stack([up_rows(rows, px) for px in some])
    down_b, near = [], []
    for py in (0, 3, 7):
        high, low = split(down_columns(columns, py))
        down_b.append(np.concatenate([high, low[:, :128]], axis=1))
        near.append(up_near(columns, py).astype(BF))
    up = []
    for py in range(8):
        one, five = up_one(columns, py)
        high, low = split(five)
        up.append(np.concatenate([one.astype(BF), high, low]))
    weights = [down_w.reshape(6, 144, 128), np.pad(up_w.reshape(6, 4, 128), ((0, 0), (0, 4), (0, 0)))]
    return (
        np.concatenate(weights, axis=1).astype(np.float32),
        np.stack(down_b),
        np.stack(up),
        np.stack(near),
        (down_w != 0).any(axis=(0, 3)).tolist(),
        (up_w != 0).any(axis=0).tolist(),
    )


def kernel(
    down_used, up_used,
    res_hbm, ff_hbm, f1_hbm, f2_hbm, f3_hbm, f4_hbm, ci_hbm, w_hbm, db_hbm, up_hbm, near_hbm,
    out_ref,
    res, ff, f1, f2, f3, f4, ci, dw, uw, db, db5, up, near,
    xt, yy, own, sb, pb, eb, xm, hs, hb, cs, cb, p0, acc,
    abuf, a5, a3, yb5, yb4, zb5, f4own, zb4, gs, gb, hs2, hb2, rs, rb, rb5, p5,
    lsem, a5send, a5recv, a3send, a3recv, bsend, brecv, dsend, drecv, msend, mrecv, y5send, y5recv, y4send, y4recv,
    z5send, z5recv, z4send, z4recv, hsend, hrecv, esend, erecv, gsend, grecv, h2send, h2recv, rsend, rrecv, r5send, r5recv,
):
    px, py = lax.axis_index("px"), lax.axis_index("py")
    z, y = px // 4, px % 4
    x, core = py // 2, py % 2
    has_left, has_right = px > 0, px < 31
    step = 2 * core - 1
    has_beside = jnp.logical_and(py + step >= 0, py + step < 8)
    beside = jnp.clip(py + step, 0, 7)
    beyond = jnp.clip(py + 2 * step, 0, 7)
    has_behind = jnp.logical_and(py - 2 * step >= 0, py - 2 * step < 8)
    behind = jnp.clip(py - 2 * step, 0, 7)
    partner = py + 1 - 2 * core
    variant = jnp.where(px == 0, 4, jnp.where(px == 31, 5, y))
    place = jnp.where(py == 0, 0, jnp.where(py == 7, 2, 1))
    lane = lax.broadcasted_iota(jnp.int32, (32, 128), 1)
    lane8 = lax.broadcasted_iota(jnp.int32, (8, 128), 1)

    def roll(tile, shift):
        if isinstance(shift, int):
            shift %= 128
            return tile if shift == 0 else pltpu.roll(tile, shift, 1)
        return pltpu.roll(tile, shift, 1)

    def only(mask, tile):
        return jnp.where(mask, tile, 0.0)

    barrier = pltpu.get_barrier_semaphore()

    def greet(**where):
        pl.semaphore_signal(barrier, inc=1, device_id=where, device_id_type=MESH)

    for d in (4, 3, 5, 2, 6, 1, 7):
        greet(px=((z + d) % 8) * 4 + y, py=py)

    local = [
        (res_hbm, res),
        (db_hbm.at[place, :, pl.ds(0, 512)], db.at[pl.ds(0, 128)]),
        (db_hbm.at[place, :, pl.ds(0, 512)], db.at[pl.ds(128, 128)]),
        (db_hbm.at[place, :, pl.ds(512, 128)], db5),
        (w_hbm.at[variant, pl.ds(0, 144)], dw),
        (w_hbm.at[variant, pl.ds(144, 8)], uw),
        (up_hbm.at[py], up),
        (f3_hbm.at[0, 0], f3),
        (f2_hbm, f2),
        (ci_hbm, ci),
        (ff_hbm, ff),
        (near_hbm.at[place], near),
    ]
    local += [(f1_hbm.at[b, x], f1.at[b]) for b in range(4)]
    local += [(f4_hbm.at[jnp.clip(2 * z - 1 + b, 0, 15), 0], f4.at[b]) for b in range(4)]
    local = [pltpu.make_async_copy(s, d, lsem.at[i]) for i, (s, d) in enumerate(local)]
    for copy in local[:5]:
        copy.start()

    for d in (4, 3, 5, 2, 6, 1, 7):
        greet(px=px, py=(py + d) % 8)
    for d in range(1, 4):
        greet(px=z * 4 + (y + d) % 4, py=py)
    left_diagonal = jnp.logical_and(has_left, has_beside)
    right_diagonal = jnp.logical_and(has_right, has_beside)

    @pl.when(has_left)
    def _():
        greet(px=px - 1, py=py)

    @pl.when(has_right)
    def _():
        greet(px=px + 1, py=py)

    @pl.when(left_diagonal)
    def _():
        greet(px=px - 1, py=beside)

    @pl.when(right_diagonal)
    def _():
        greet(px=px + 1, py=beside)

    for copy in local[5:]:
        copy.start()

    def send(src, dst, ssem, rsem, **where):
        return pltpu.make_async_remote_copy(
            src_ref=src, dst_ref=dst, send_sem=ssem, recv_sem=rsem, device_id=where, device_id_type=MESH
        )

    nothing = jnp.zeros((32, 128), F32)
    nothing8 = jnp.zeros((8, 128), F32)
    for end in (0, 9):
        zb5[end] = nothing8
        for i in range(2):
            eb[end, i] = nothing

    for side, missing in ((0, px == 0), (1, px == 31)):

        @pl.when(missing)
        def _(side=side):
            for i in range(3):
                pb[side, i] = nothing
                hb2[side, i] = nothing8
            hb[side] = nothing
            for i in range(6):
                gb[side, i] = nothing8

    for side, missing in ((0, z == 0), (1, z == 7)):

        @pl.when(missing)
        def _(side=side):
            for i in range(3):
                zb4[side, i] = nothing8

    diag = (left_diagonal, has_beside, right_diagonal)
    for i in range(3):

        @pl.when(jnp.logical_not(diag[i]))
        def _(i=i):
            cb[i] = nothing

    local[0].wait()
    for f in range(16):
        xt[f] = res[pl.ds(f, 32, stride=16), :]
    rows = xt[...].reshape(512, 128)
    high = rows.astype(BF)
    low = (rows - high.astype(F32)).astype(BF)
    both = jnp.concatenate([high, low], axis=1)
    for i in range(1, 5):
        local[i].wait()
    yy[:, :256] = jnp.dot(both, db[:, :256], preferred_element_type=F32)
    yy[:, :128] += jnp.dot(high, db5[...], preferred_element_type=F32)

    def packed(t):
        at = 128 * GROUP_OF[t]
        total = None
        for f in range(16):
            if down_used[t][f]:
                term = yy[32 * f : 32 * f + 32, at : at + 128] * dw[16 * t + f : 16 * t + f + 1, :]
                total = term if total is None else total + term
        return total

    eb[py + 1, 0] = packed(0)
    a5[py] = eb[py + 1, 0, pl.ds(pl.multiple_of(8 * x, 8), 8), :]
    pl.semaphore_wait(
        barrier,
        17
        + jnp.where(has_left, 1, 0)
        + jnp.where(has_right, 1, 0)
        + jnp.where(left_diagonal, 1, 0)
        + jnp.where(right_diagonal, 1, 0),
    )

    sent = []

    def begin(copy):
        copy.start()
        sent.append(copy)

    FAR = (4, 3, 5, 2, 6, 1, 7)

    def to_five(d, me):
        peer = (me + d) % 8
        group = pl.multiple_of(8 * (peer // 2), 8)
        return send(eb.at[py + 1, 0, pl.ds(group, 8)], a5.at[me], a5send.at[d - 1], a5recv.at[me], px=px, py=peer)

    def to_three(d, me):
        peer = (me + d) % 8
        return send(abuf.at[peer // 2], a3.at[me], a3send.at[d - 1], a3recv.at[me], px=px, py=peer)

    for d in FAR:
        begin(to_five(d, py))

    yy[:, 256:] = jnp.dot(both, db[:, 256:], preferred_element_type=F32)
    for t in range(1, 4):
        tile = packed(t)
        own[t - 1] = tile
        for c in range(4):
            abuf[c, t - 1] = tile[8 * c : 8 * c + 8]
    a3[py] = abuf[x]
    for d in FAR:
        begin(to_three(d, py))
    for t in range(4, 9):
        own[t - 1] = packed(t)
    sb[0, 0] = own[0]
    sb[1, 0] = own[0]
    sb[0, 1] = own[3]
    sb[1, 1] = own[7]
    sb[0, 2] = xt[0]
    sb[1, 2] = xt[15]

    def left_copy(src, dst, ssem, rsem):
        return send(src.at[0], dst.at[1], ssem.at[0], rsem.at[1], px=px - 1, py=py)

    def right_copy(src, dst, ssem, rsem):
        return send(src.at[1], dst.at[0], ssem.at[1], rsem.at[0], px=px + 1, py=py)

    def start_rows(*refs):
        @pl.when(has_left)
        def _():
            left_copy(*refs).start()

        @pl.when(has_right)
        def _():
            right_copy(*refs).start()

    def got_rows(src, dst, ssem, rsem):
        @pl.when(has_left)
        def _():
            send(src.at[1], dst.at[0], ssem.at[1], rsem.at[0], px=px - 1, py=py).wait_recv()

        @pl.when(has_right)
        def _():
            send(src.at[0], dst.at[1], ssem.at[0], rsem.at[1], px=px + 1, py=py).wait_recv()

    def sent_rows(*refs):
        @pl.when(has_left)
        def _():
            left_copy(*refs).wait_send()

        @pl.when(has_right)
        def _():
            right_copy(*refs).wait_send()

    b_refs = (sb, pb, bsend, brecv)
    start_rows(*b_refs)

    for d in range(1, 8):
        to_five(d, (py + 8 - d) % 8).wait_recv()
    five, fours = None, [None] * 3
    for p in range(8):
        tile = a5[p]
        term = only(((lane8 - 4 * p + 1) & 31) < 6, roll(tile, 4 * p - 1))
        five = term if five is None else five + term
        close = ((lane8 - 8 * p + 1) & 63) < 10
        for m in range(3):
            term = only(close, roll(tile, 8 * p - 1 - LANES_FOUR[m]))
            fours[m] = term if fours[m] is None else fours[m] + term
    yb5[y] = five
    for m in range(3):
        yb4[y, m] = fours[m]

    def to_y(buffer, ssem, rsem, d, slot):
        return send(buffer.at[slot], buffer.at[slot], ssem.at[d - 1], rsem.at[slot], px=z * 4 + (y + d) % 4, py=py)

    for d in (2, 1, 3):
        begin(to_y(yb5, y5send, y5recv, d, y))
    for d in (2, 1, 3):
        begin(to_y(yb4, y4send, y4recv, d, y))

    for d in range(1, 8):
        to_three(d, (py + 8 - d) % 8).wait_recv()
    rows_three = []
    for s in range(4):
        total = None
        for p in range(8):
            close = jnp.logical_and(lane8 >= 16 * p - 1, lane8 <= 16 * p + 16)
            term = only(close, roll(a3[p, 0], 16 * p - 1 - 32 * s))
            total = term if total is None else total + term
        rows_three.append(total)
    rows_two = []
    for r in range(6):
        half, u = next((h, ROWS_TWO[h].index(r)) for h in range(2) if r in ROWS_TWO[h])
        pair = [None, None]
        for p in range(8):
            turned = roll(a3[p, 1 + half], 32 * p - 1 - 42 * u)
            first = 32 * (p % 4) - 1
            close = jnp.logical_and(lane8 >= first, lane8 <= first + 33)
            term = only(close, turned)
            pair[p // 4] = term if pair[p // 4] is None else pair[p // 4] + term
            if p == 3:
                pair[1] = only(lane8 == 0, turned)
            if p == 4:
                pair[0] = pair[0] + only(lane8 == 127, turned)
        rows_two.append(pair)
    for side in range(2):
        for i in range(2):
            gs[side, i] = rows_three[2 * side + i]
            for t in range(2):
                gs[side, 2 + 2 * i + t] = rows_two[4 * side + i][t]
    g_refs = (gs, gb, gsend, grecv)
    start_rows(*g_refs)

    got_rows(*b_refs)
    mine = own[0]
    across = jnp.where(lane < 64, roll(pb[0, 0], 64), roll(pb[1, 0], 64))
    inside = jnp.logical_or((lane & 63) < 50, (lane & 63) > 61)
    mine = mine + only(inside, across)
    corner = jnp.where(lane < 28, roll(pb[0, 2], 27), roll(pb[1, 2], 29))
    eb[py + 1, 1] = jnp.where(jnp.logical_and(lane >= 26, lane < 30), corner, mine)
    xm[core, 0] = own[3] + pb[0, 1]
    for m in range(1, 4):
        xm[core, m] = own[3 + m]
    xm[core, 4] = own[7] + pb[1, 1]

    def to_partner(slot):
        return send(xm.at[slot], xm.at[slot], msend, mrecv, px=px, py=partner)

    def edge_copy(i, slot, peer):
        return send(eb.at[slot + 1], eb.at[slot + 1], dsend.at[i], drecv.at[slot], px=px, py=peer)

    @pl.when(has_beside)
    def _():
        edge_copy(0, py, beside).start()
        edge_copy(1, py, beyond).start()

    begin(edge_copy(2, py, partner))
    begin(to_partner(core))

    for d in range(1, 4):
        to_y(yb5, y5send, y5recv, d, (y + 4 - d) % 4).wait_recv()
    zb5[z + 1] = (yb5[0] + yb5[1]) + (yb5[2] + yb5[3])

    def to_z(d, slot):
        return send(zb5.at[slot + 1], zb5.at[slot + 1], z5send.at[d - 1], z5recv.at[slot], px=((z + d) % 8) * 4 + y, py=py)

    for d in FAR:
        begin(to_z(d, z))
    for d in range(1, 4):
        to_y(yb4, y4send, y4recv, d, (y + 4 - d) % 4).wait_recv()
    for m in range(3):
        f4own[m] = (yb4[0, m] + yb4[1, m]) + (yb4[2, m] + yb4[3, m])

    def z4_down():
        return send(f4own, zb4.at[1], z4send.at[0], z4recv.at[1], px=px - 4, py=py)

    def z4_up():
        return send(f4own, zb4.at[0], z4send.at[1], z4recv.at[0], px=px + 4, py=py)

    @pl.when(z > 0)
    def _():
        z4_down().start()

    @pl.when(z < 7)
    def _():
        z4_up().start()

    def solve(windows, factor):
        return jnp.dot(windows.astype(BF), factor, preferred_element_type=F32)

    def window(at, shifted, halo):
        parts = [jnp.where(at == 0, halo(0), shifted[0])]
        for j in range(1, 4):
            parts.append(jnp.where(at <= 2 * j - 2, shifted[j - 1], jnp.where(at <= 2 * j, halo(j), shifted[j])))
        last = jnp.where(at <= 6, shifted[3], halo(4))
        return jnp.concatenate(parts + [last[:, :8]], axis=1)

    def lifted(tiles, table):
        count = 32 * len(tiles)
        fine = jnp.concatenate(tiles, axis=0)
        top = fine.astype(BF)
        rest = (fine - top.astype(F32)).astype(BF)
        product = jnp.dot(jnp.concatenate([top, rest], axis=0), table, preferred_element_type=F32)
        product = product[:count] + product[count:]
        return [product[32 * i : 32 * i + 32] for i in range(len(tiles))]

    got_rows(*g_refs)
    for side in range(2):
        for i in range(2):
            rows_three[2 * side + i] = rows_three[2 * side + i] + gb[side, i]
            rows_two[4 * side + i] = [rows_two[4 * side + i][t] + gb[side, 2 + 2 * i + t] for t in range(2)]
    local[7].wait()
    shifted = [roll(rows_three[k], 2 * k + 1) for k in range(4)]
    solved = solve(window(lane8, shifted, lambda j: nothing8), f3[...])
    three = [solved[:, :128], solved[:, 128:]]
    local[8].wait()
    two = []
    for b in range(2):
        turned = [[roll(rows_two[2 * b + k][t], 2 * k + 1) for k in range(4)] for t in range(2)]

        def right_of(j, turned=turned):
            return only(lane8 == 2 * j - 1, turned[1][j - 1]) if j > 0 else nothing8

        def left_of(j, turned=turned):
            return only(lane8 == 2 * j, turned[0][j]) if j < 4 else nothing8

        left_tile = solve(window(lane8, turned[0], right_of), f2[b, 0])
        right_tile = solve(window(lane8, turned[1], left_of), f2[b, 1])
        for h in range(2):
            at = slice(128 * h, 128 * h + 128)
            two.append((left_tile[:, at], right_tile[:, at]))
    for side in range(2):
        hs2[side, 0] = three[side]
        for t in range(2):
            hs2[side, 1 + t] = two[3 * side][t]
    h2_refs = (hs2, hb2, h2send, h2recv)
    start_rows(*h2_refs)

    edge_copy(2, partner, partner).wait_recv()

    @pl.when(has_beside)
    def _():
        edge_copy(0, beside, beside).wait_recv()

    @pl.when(has_behind)
    def _():
        edge_copy(1, behind, behind).wait_recv()

    to_partner(1 - core).wait_recv()
    left_edge, first_edge, second_edge, right_edge = (eb[2 * x + i, 1] for i in range(4))
    even = (lane & 1) == 0

    def edges(n):
        mid = jnp.where(even, second_edge, roll(first_edge, -n))
        outer = jnp.where(even, right_edge, roll(left_edge, -n))
        halo = jnp.where(even, first_edge + roll(left_edge, -n), right_edge + roll(second_edge, -n))
        return mid, outer, halo

    edges_of = {2: edges(4), 3: edges(6)}
    rows_one = []
    for r in range(10):
        m, h = divmod(r, 2)
        if h == 0:
            main = jnp.where(lane < 64, xm[0, m], roll(xm[1, m], 64))
        else:
            main = jnp.where(lane < 64, roll(xm[0, m], 64), xm[1, m])
        at, last = edge_lanes(r)
        mid, outer, _ = edges_of[(last - at) // 2]
        main = main + only(jnp.logical_or(lane == 63, lane == 64), roll(mid, 63 - at))
        main = main + only(jnp.logical_or(lane == 127, lane == 0), roll(outer, 127 - at))
        rows_one.append(main)
    halo_two, halo_three = edges_of[2][2], edges_of[3][2]
    halos = jnp.where(
        lane < 4,
        roll(halo_two, -18),
        jnp.where(lane < 10, roll(halo_three, -46), jnp.where(lane < 16, roll(halo_three, -104), roll(halo_two, -66))),
    )
    one = []
    for b in range(4):
        local[12 + b].wait()
        turned = [roll(rows_one[2 * b + k], 2 * k + 1) for k in range(4)]
        side = roll(halos, -4 * b)
        solved = solve(window(lane, turned, lambda j, side=side: side), f1[b])
        one += [solved[:, :128], solved[:, 128:]]
    hs[0] = one[0]
    hs[1] = one[7]
    h_refs = (hs, hb, hsend, hrecv)
    start_rows(*h_refs)
    column = nothing
    for r in range(8):
        column = jnp.where(lane == r, roll(one[r], r + core), column)
    cs[...] = column

    def to_side(d):
        return send(cs, cb.at[1 - d], esend.at[1 - d], erecv.at[1 - d], px=px + d, py=beside)

    for d in (-1, 1, 0):

        @pl.when(diag[1 + d])
        def _(d=d):
            to_side(d).start()

    @pl.when(z > 0)
    def _():
        send(f4own, zb4.at[0], z4send.at[1], z4recv.at[0], px=px - 4, py=py).wait_recv()

    @pl.when(z < 7)
    def _():
        send(f4own, zb4.at[1], z4send.at[0], z4recv.at[1], px=px + 4, py=py).wait_recv()

    quads = (zb4[0, 1], zb4[0, 2] + f4own[0], f4own[1], f4own[2] + zb4[1, 0], zb4[1, 1])
    four = []
    for b in range(4):
        local[16 + b].wait()
        first, second = quads[b], quads[b + 1]
        v0 = jnp.where(
            lane8 <= 64,
            only(lane8 >= 1, roll(first, 1)),
            only(lane8 >= 67, roll(first, 3)),
        )
        v1 = jnp.where(
            lane8 <= 2,
            roll(first, 3),
            jnp.where(lane8 <= 68, only(lane8 >= 5, roll(second, 5)), only(lane8 >= 71, roll(second, 7))),
        )
        v2 = only(lane8 <= 6, roll(second, 7))
        four.append(solve(jnp.concatenate([v0, v1, v2[:, :8]], axis=1), f4[b]))

    got_rows(*h2_refs)
    three = [hb2[0, 0]] + three + [hb2[1, 0]]
    two = [(hb2[0, 1], hb2[0, 2])] + two + [(hb2[1, 1], hb2[1, 2])]
    for c in range(4):

        def moved(tile, shift, width, c=c):
            return roll(tile, (shift + 1 - width * 2 * c + 512 - width * core) % 128)

        for half in range(2):
            pieces = []
            for u in range(3):
                row = two[3 * half + u]
                tile = row[c // 2]
                if c == 1:
                    tile = jnp.where(lane8 == 0, row[1], row[0])
                if c == 2:
                    tile = jnp.where(lane8 == 127, row[0], row[1])
                pieces.append(moved(tile, 42 * u, 32))
            rs[c, half] = jnp.where(lane8 < 42, pieces[0], jnp.where(lane8 < 84, pieces[1], pieces[2]))
        pieces = [moved(three[s], 32 * s, 16) for s in range(4)]
        rs[c, 2] = jnp.where(
            lane8 < 64, jnp.where(lane8 < 32, pieces[0], pieces[1]), jnp.where(lane8 < 96, pieces[2], pieces[3])
        )
        pieces = [moved(four[b], 10 * b, 8) for b in range(4)]
        low_lane = lane8 & 63
        rs[c, 3] = jnp.where(
            low_lane < 20,
            jnp.where(low_lane < 10, pieces[0], pieces[1]),
            jnp.where(low_lane < 30, pieces[2], pieces[3]),
        )
    rb[x] = rs[x]

    def to_chip(d, me):
        peer = (me + d) % 4
        return send(rs.at[peer], rb.at[me], rsend.at[d - 1], rrecv.at[me], px=px, py=2 * peer + core)

    for d in (2, 1, 3):
        begin(to_chip(d, x))

    before, after = eb[py, 0], eb[py + 2, 0]
    corner_before, corner_after = eb[py, 1], eb[py + 2, 1]
    facing = jnp.where(even, before, after)
    corners = jnp.where(even, corner_before, corner_after)
    halos = jnp.where(
        lane < 2,
        roll(corners, -26),
        jnp.where(lane < 18, roll(facing, -46), jnp.where(lane < 34, roll(facing, -94), roll(corners, 6))),
    )
    local[10].wait()
    for b in range(8):
        tiles = []
        for k in range(4):
            at = 2 * b + k
            tile = pb[0, 2] if at == 0 else pb[1, 2] if at == 17 else xt[at - 1]
            tiles.append(roll(tile, 2 * k + 1))
        side = roll(halos, -4 * b)
        solved = solve(window(lane, tiles, lambda j, side=side: side), ff[b, 0])
        p0[2 * b] = solved[:, :128]
        p0[2 * b + 1] = solved[:, 128:]

    for d in range(1, 8):
        to_z(d, (z + 8 - d) % 8).wait_recv()
    local[9].wait()
    down = [roll(zb5[i + 1], -32) if i < 8 else nothing8 for i in range(0, 10, 2)]
    rise = [nothing8] + [roll(zb5[i + 1], 32) for i in range(1, 8, 2)]
    flat = [
        jnp.where(lane8 < 96, down[j], down[j + 1]) + jnp.where(lane8 >= 32, rise[j + 1], rise[j]) for j in range(4)
    ]
    solved = solve(jnp.concatenate(flat, axis=1), ci[...])
    p5[0] = nothing8
    p5[5] = nothing8
    for j in range(4):
        p5[j + 1] = solved[:, 128 * j : 128 * j + 128]
    odd = z % 2
    lead = (z + odd) // 2
    edge = 32 + 64 * odd
    rb5[x] = jnp.where(lane8 < edge, roll(p5[lead], edge), roll(p5[lead + 1], edge))

    def to_chip5(d, me):
        peer = (me + d) % 4
        return send(rb5.at[me], rb5.at[me], r5send.at[d - 1], r5recv.at[me], px=px, py=2 * peer + core)

    for d in (2, 1, 3):
        begin(to_chip5(d, x))

    got_rows(*h_refs)
    for d in (-1, 0, 1):

        @pl.when(diag[1 + d])
        def _(d=d):
            send(cs, cb.at[1 + d], esend.at[1 + d], erecv.at[1 + d], px=px + d, py=beside).wait_recv()

    local[6].wait()
    local[11].wait()
    one = [hb[0]] + one + [hb[1]]
    at_lane = 127 * (1 - core)
    for r in range(10):
        source, from_lane = (0, 7) if r == 0 else (2, 0) if r == 9 else (1, r - 1)
        one[r] = jnp.where(lane == at_lane, roll(cb[source], (at_lane - from_lane + 128) % 128), one[r])
    one = lifted(one, up[0:128, :])
    for d in range(1, 4):
        to_chip(d, (x + 4 - d) % 4).wait_recv()
    back = [rb[:, t].reshape(32, 128) for t in range(4)]
    two = [only(jnp.logical_and(lane >= 42 * u, lane < 42 * u + 34), back[h]) for h in range(2) for u in range(3)]
    three = [only((lane // 32) == s, back[2]) for s in range(4)]
    four = [
        only(jnp.logical_and(lane >= 64 * h + 10 * b, lane < 64 * h + 10 * b + 10), back[3])
        for b in range(4)
        for h in range(2)
    ]
    two = lifted(two, near[0:128, :])
    three = lifted(three, near[128:256, :])
    four = lifted(four, near[256:384, :])
    local[5].wait()
    terms = one + two + three + four
    for f in range(16):
        total = p0[f]
        for r in range(28):
            if up_used[r][f]:
                total = total + uw[r // 8, 16 * (r % 8) + f] * terms[r]
        acc[f] = total

    for d in range(1, 4):
        to_chip5(d, (x + 4 - d) % 4).wait_recv()
    five = rb5[...].reshape(32, 128)
    full = jnp.concatenate([only((lane // 32) == s, five) for s in range(4)], axis=0)
    top = full.astype(BF)
    rest = (full - top.astype(F32)).astype(BF)
    product = jnp.dot(jnp.concatenate([top, rest], axis=0), up[128:256, :], preferred_element_type=F32)
    product = product[:128] + product[128:] + jnp.dot(top, up[256:384, :], preferred_element_type=F32)
    for f in range(16):
        total = acc[f]
        for s in range(4):
            if up_used[28 + s][f]:
                total = total + uw[3, 16 * (4 + s) + f] * product[32 * s : 32 * s + 32]
        out_ref[pl.ds(f, 32, stride=16), :] = total

    for copy in sent:
        copy.wait_send()
    for refs in (b_refs, g_refs, h2_refs, h_refs):
        sent_rows(*refs)

    @pl.when(has_beside)
    def _():
        edge_copy(0, py, beside).wait_send()
        edge_copy(1, py, beyond).wait_send()

    @pl.when(z > 0)
    def _():
        z4_down().wait_send()

    @pl.when(z < 7)
    def _():
        z4_up().wait_send()

    for d in (-1, 0, 1):

        @pl.when(diag[1 + d])
        def _(d=d):
            to_side(d).wait_send()


def per_device(residual, fine, one, two, three, four, inverse):
    weights, down_b, up, near, down_used, up_used = tables()

    def tiles(*lead):
        return pltpu.VMEM(lead + (32, 128), F32)

    def small(*lead):
        return pltpu.VMEM(lead + (8, 128), F32)

    dma = pltpu.SemaphoreType.DMA
    out = pl.pallas_call(
        functools.partial(kernel, down_used, up_used),
        out_shape=jax.ShapeDtypeStruct((512, 128), F32),
        in_specs=[pl.BlockSpec(memory_space=pltpu.HBM)] * 11,
        out_specs=pl.BlockSpec(memory_space=pltpu.VMEM),
        scratch_shapes=[
            pltpu.VMEM((512, 128), F32),
            pltpu.VMEM((8, 1, 520, 256), BF),
            pltpu.VMEM((4, 520, 256), BF),
            pltpu.VMEM((2, 2, 520, 256), BF),
            pltpu.VMEM((520, 256), BF),
            pltpu.VMEM((4, 264, 128), BF),
            pltpu.VMEM((512, 512), BF),
            pltpu.VMEM((144, 128), F32),
            pltpu.SMEM((8, 128), F32),
            pltpu.VMEM((256, 512), BF),
            pltpu.VMEM((128, 128), BF),
            pltpu.VMEM((384, 128), BF),
            pltpu.VMEM((384, 128), BF),
            tiles(16),
            pltpu.VMEM((512, 512), F32),
            tiles(8),
            tiles(2, 3),
            tiles(2, 3),
            tiles(10, 2),
            tiles(2, 5),
            tiles(2),
            tiles(2),
            tiles(),
            tiles(3),
            tiles(16),
            tiles(16),
            small(4, 3),
            small(8),
            small(8, 3),
            small(4),
            small(4, 3),
            small(10),
            small(3),
            small(2, 3),
            small(2, 6),
            small(2, 6),
            small(2, 3),
            small(2, 3),
            small(4, 4),
            small(4, 4),
            small(4),
            small(6),
            dma((20,)),
        ]
        + [
            dma if n == 0 else dma((n,))
            for n in (7, 8, 7, 8, 2, 2, 3, 8, 0, 0, 3, 4, 3, 4, 7, 8, 2, 2, 2, 2, 3, 3, 2, 2, 2, 2, 3, 4, 3, 4)
        ],
        compiler_params=pltpu.CompilerParams(
            collective_id=0, has_side_effects=True, vmem_limit_bytes=56147968
        ),
    )(
        residual.reshape(512, 128), fine, one, two, three, four, inverse,
        jnp.asarray(weights), jnp.asarray(down_b), jnp.asarray(up), jnp.asarray(near),
    )
    return out.reshape(32, 16, 128)


def solution(mesh):
    placed = (
        P(None, "px", "py"),
        P("px", "py", None, None),
        P("px", None, None, None),
        P("px", None, None, None),
        P("px", None, None, None),
        P(),
        P(),
    )
    return jax.shard_map(
        per_device, mesh=mesh, in_specs=placed, out_specs=P(None, "px", "py"), check_vma=False
    )
```

time: 30.7 us -> 27 us (0.88)
  the two profiles are of different devices: /device:TPU:32 before, /device:TPU:24 now
where the time goes in v2:
time: 27 us; the launch traced here: 26.9 us
  Pallas kernels  26.2 us (97%)
  local copies, waits for them, and re-layouts  0.71 us (3%)
    pallas_call x1, Pallas kernels, per_device(): pl.pallas_call(functools.partial(kernel, down_used, up_used), out_shape=j...  26.2 us
    unnamed x1, local copies, waits for them, and re-layouts  0.71 us

profile of v2, /device:TPU:24, one launch (start us, length us, event | category | flops | bytes accessed | tf_op | source)
XLA Modules:
  0.0 26.9 jit_solution(10442540169236288852)
XLA Ops:
  0.0 26.2 %shard_map.109 = f32[512,128]{1,0:T(8,128)S(1)} custom-call(f32[512,128]{1,0:T(8,128)} %bitcast.3, bf16[8,1,520,256]{3,2,1,0:T(8,128)(2,1)} %ff_hbm.1, bf16[4,4,520,256]{3,2,1,0:T(8,128)(2,1)} %f1_hbm.1, bf16[2,2,520,256]{3,2,1,0:T(8,128)(2,1)} %f2_hbm.1, bf16[1,1,520,256]{3,2,1,0:T(8,128)(2,1)} %f3_hbm.1, bf16[16,1,264,128]{3,2,1,0:T(8,128)(2,1)} %f4_hbm.1, ...), custom_call_target="tpu_custom_call" | custom-call | tf_op jit(solution)/shard_map/pallas_call | solution.py:818
  26.2 0.7 %copy.13 = f32[32,16,128]{2,1,0:T(8,128)} copy(f32[32,16,128]{2,1,0:T(8,128)S(1)} %bitcast.2) | data formatting | bytes 524288

commit v3 on v2

--- a/solution.py
+++ b/solution.py
@@ -168,7 +168,7 @@
     xt, yy, own, sb, pb, eb, xm, hs, hb, cs, cb, p0, acc,
     abuf, a5, a3, yb5, yb4, zb5, f4own, zb4, gs, gb, hs2, hb2, rs, rb, rb5, p5,
     lsem, a5send, a5recv, a3send, a3recv, bsend, brecv, dsend, drecv, msend, mrecv, y5send, y5recv, y4send, y4recv,
-    z5send, z5recv, z4send, z4recv, hsend, hrecv, esend, erecv, gsend, grecv, h2send, h2recv, rsend, rrecv, r5send, r5recv,
+    z5send, z5recv, z4send, z4recv, hsend, hrecv, esend, erecv, gsend, grecv, h2send, h2recv, rsend, rrecv, r5send, r5recv, zs,
 ):
     px, py = lax.axis_index("px"), lax.axis_index("py")
     z, y = px // 4, px % 4
@@ -200,7 +200,7 @@
     def greet(**where):
         pl.semaphore_signal(barrier, inc=1, device_id=where, device_id_type=MESH)
 
-    for d in (4, 3, 5, 2, 6, 1, 7):
+    for d in (1, 7):
         greet(px=((z + d) % 8) * 4 + y, py=py)
 
     local = [
@@ -238,17 +238,6 @@
     def _():
         greet(px=px + 1, py=py)
 
-    @pl.when(left_diagonal)
-    def _():
-        greet(px=px - 1, py=beside)
-
-    @pl.when(right_diagonal)
-    def _():
-        greet(px=px + 1, py=beside)
-
-    for copy in local[5:]:
-        copy.start()
-
     def send(src, dst, ssem, rsem, **where):
         return pltpu.make_async_remote_copy(
             src_ref=src, dst_ref=dst, send_sem=ssem, recv_sem=rsem, device_id=where, device_id_type=MESH
@@ -311,12 +300,13 @@
     a5[py] = eb[py + 1, 0, pl.ds(pl.multiple_of(8 * x, 8), 8), :]
     pl.semaphore_wait(
         barrier,
-        17
-        + jnp.where(has_left, 1, 0)
-        + jnp.where(has_right, 1, 0)
-        + jnp.where(left_diagonal, 1, 0)
-        + jnp.where(right_diagonal, 1, 0),
+        12 + jnp.where(has_left, 1, 0) + jnp.where(has_right, 1, 0),
     )
+
+    def pass_on(i):
+        for d in (1, 7):
+            peer = {"px": ((z + d) % 8) * 4 + y, "py": py}
+            pl.semaphore_signal(zs.at[i], inc=1, device_id=peer, device_id_type=MESH)
 
     sent = []
 
@@ -337,6 +327,9 @@
 
     for d in FAR:
         begin(to_five(d, py))
+    pass_on(0)
+    for copy in local[5:]:
+        copy.start()
 
     yy[:, 256:] = jnp.dot(both, db[:, 256:], preferred_element_type=F32)
     for t in range(1, 4):
@@ -347,6 +340,8 @@
     a3[py] = abuf[x]
     for d in FAR:
         begin(to_three(d, py))
+    pl.semaphore_wait(zs.at[0], 2)
+    pass_on(1)
     for t in range(4, 9):
         own[t - 1] = packed(t)
     sb[0, 0] = own[0]
@@ -391,6 +386,8 @@
 
     b_refs = (sb, pb, bsend, brecv)
     start_rows(*b_refs)
+    pl.semaphore_wait(zs.at[1], 2)
+    pass_on(2)
 
     for d in range(1, 8):
         to_five(d, (py + 8 - d) % 8).wait_recv()
@@ -481,6 +478,7 @@
     def to_z(d, slot):
         return send(zb5.at[slot + 1], zb5.at[slot + 1], z5send.at[d - 1], z5recv.at[slot], px=((z + d) % 8) * 4 + y, py=py)
 
+    pl.semaphore_wait(zs.at[2], 2)
     for d in FAR:
         begin(to_z(d, z))
     for d in range(1, 4):
@@ -868,7 +866,8 @@
         + [
             dma if n == 0 else dma((n,))
             for n in (7, 8, 7, 8, 2, 2, 3, 8, 0, 0, 3, 4, 3, 4, 7, 8, 2, 2, 2, 2, 3, 3, 2, 2, 2, 2, 3, 4, 3, 4)
-        ],
+        ]
+        + [pltpu.SemaphoreType.REGULAR((3,))],
         compiler_params=pltpu.CompilerParams(
             collective_id=0, has_side_effects=True, vmem_limit_bytes=56147968
         ),

time: 27 us -> 26.1 us (0.967)
  the two profiles are of different devices: /device:TPU:24 before, /device:TPU:32 now
where the time goes in v3:
time: 26.1 us; the launch traced here: 26 us
  Pallas kernels  25.3 us (97%)
  local copies, waits for them, and re-layouts  0.71 us (3%)
    pallas_call x1, Pallas kernels, per_device(): pl.pallas_call(functools.partial(kernel, down_used, up_used), out_shape=j...  25.3 us
    unnamed x1, local copies, waits for them, and re-layouts  0.71 us

profile of v3, /device:TPU:32, one launch (start us, length us, event | category | flops | bytes accessed | tf_op | source)
XLA Modules:
  0.0 26.0 jit_solution(10837993411652067230)
XLA Ops:
  0.0 25.3 %shard_map.109 = f32[512,128]{1,0:T(8,128)S(1)} custom-call(f32[512,128]{1,0:T(8,128)} %bitcast.3, bf16[8,1,520,256]{3,2,1,0:T(8,128)(2,1)} %ff_hbm.1, bf16[4,4,520,256]{3,2,1,0:T(8,128)(2,1)} %f1_hbm.1, bf16[2,2,520,256]{3,2,1,0:T(8,128)(2,1)} %f2_hbm.1, bf16[1,1,520,256]{3,2,1,0:T(8,128)(2,1)} %f3_hbm.1, bf16[16,1,264,128]{3,2,1,0:T(8,128)(2,1)} %f4_hbm.1, ...), custom_call_target="tpu_custom_call" | custom-call | tf_op jit(solution)/shard_map/pallas_call | solution.py:816
  25.3 0.7 %copy.13 = f32[32,16,128]{2,1,0:T(8,128)} copy(f32[32,16,128]{2,1,0:T(8,128)S(1)} %bitcast.2) | data formatting | bytes 524288

commit v4 on v3

--- a/solution.py
+++ b/solution.py
@@ -166,9 +166,9 @@
     out_ref,
     res, ff, f1, f2, f3, f4, ci, dw, uw, db, db5, up, near,
     xt, yy, own, sb, pb, eb, xm, hs, hb, cs, cb, p0, acc,
-    abuf, a5, a3, yb5, yb4, zb5, f4own, zb4, gs, gb, hs2, hb2, rs, rb, rb5, p5,
+    abuf, a5, a3, yb5, yb4, zb5, f4own, zb4, gs, gb, ns, nb, rs, rb, rb5, p5,
     lsem, a5send, a5recv, a3send, a3recv, bsend, brecv, dsend, drecv, msend, mrecv, y5send, y5recv, y4send, y4recv,
-    z5send, z5recv, z4send, z4recv, hsend, hrecv, esend, erecv, gsend, grecv, h2send, h2recv, rsend, rrecv, r5send, r5recv, zs,
+    z5send, z5recv, z4send, z4recv, hsend, hrecv, esend, erecv, gsend, grecv, nsend, nrecv, rsend, rrecv, r5send, r5recv, zs,
 ):
     px, py = lax.axis_index("px"), lax.axis_index("py")
     z, y = px // 4, px % 4
@@ -256,7 +256,8 @@
         def _(side=side):
             for i in range(3):
                 pb[side, i] = nothing
-                hb2[side, i] = nothing8
+            for i in range(4):
+                nb[side, i] = nothing8
             hb[side] = nothing
             for i in range(6):
                 gb[side, i] = nothing8
@@ -544,12 +545,34 @@
         for h in range(2):
             at = slice(128 * h, 128 * h + 128)
             two.append((left_tile[:, at], right_tile[:, at]))
+
+    def moved(tile, c, shift, width):
+        return roll(tile, (shift + 1 - width * 2 * c + 512 - width * core) % 128)
+
+    def moved_two(row, c, shift):
+        tile = row[c // 2]
+        if c == 1:
+            tile = jnp.where(lane8 == 0, row[1], row[0])
+        if c == 2:
+            tile = jnp.where(lane8 == 127, row[0], row[1])
+        return moved(tile, c, shift, 32)
+
     for side in range(2):
-        hs2[side, 0] = three[side]
-        for t in range(2):
-            hs2[side, 1 + t] = two[3 * side][t]
-    h2_refs = (hs2, hb2, h2send, h2recv)
-    start_rows(*h2_refs)
+        for c in range(4):
+            ns[side, c] = jnp.where(lane8 < 64, moved_two(two[3 * side], c, 0), moved(three[side], c, 64, 16))
+
+    def to_near(side, c, me):
+        return send(
+            ns.at[side, c], nb.at[1 - side, me], nsend.at[side, c], nrecv.at[1 - side, me],
+            px=px + 2 * side - 1, py=2 * c + core,
+        )
+
+    for side, there in ((0, has_left), (1, has_right)):
+
+        @pl.when(there)
+        def _(side=side):
+            for c in range(4):
+                to_near(side, c, x).start()
 
     edge_copy(2, partner, partner).wait_recv()
 
@@ -641,32 +664,14 @@
         v2 = only(lane8 <= 6, roll(second, 7))
         four.append(solve(jnp.concatenate([v0, v1, v2[:, :8]], axis=1), f4[b]))
 
-    got_rows(*h2_refs)
-    three = [hb2[0, 0]] + three + [hb2[1, 0]]
-    two = [(hb2[0, 1], hb2[0, 2])] + two + [(hb2[1, 1], hb2[1, 2])]
     for c in range(4):
-
-        def moved(tile, shift, width, c=c):
-            return roll(tile, (shift + 1 - width * 2 * c + 512 - width * core) % 128)
-
-        for half in range(2):
-            pieces = []
-            for u in range(3):
-                row = two[3 * half + u]
-                tile = row[c // 2]
-                if c == 1:
-                    tile = jnp.where(lane8 == 0, row[1], row[0])
-                if c == 2:
-                    tile = jnp.where(lane8 == 127, row[0], row[1])
-                pieces.append(moved(tile, 42 * u, 32))
-            rs[c, half] = jnp.where(lane8 < 42, pieces[0], jnp.where(lane8 < 84, pieces[1], pieces[2]))
-        pieces = [moved(three[s], 32 * s, 16) for s in range(4)]
+        pieces = [moved_two(two[u], c, 42 * u) for u in range(3)]
+        rs[c, 0] = jnp.where(lane8 < 42, pieces[0], jnp.where(lane8 < 84, pieces[1], pieces[2]))
+        pieces = [moved(three[s], c, 32 * s + 32, 16) for s in range(2)]
+        rs[c, 1] = jnp.where(lane8 < 84, jnp.where(lane8 < 64, pieces[0], pieces[1]), moved_two(two[3], c, 84))
+        pieces = [moved(four[b], c, 10 * b, 8) for b in range(4)]
+        low_lane = lane8 & 63
         rs[c, 2] = jnp.where(
-            lane8 < 64, jnp.where(lane8 < 32, pieces[0], pieces[1]), jnp.where(lane8 < 96, pieces[2], pieces[3])
-        )
-        pieces = [moved(four[b], 10 * b, 8) for b in range(4)]
-        low_lane = lane8 & 63
-        rs[c, 3] = jnp.where(
             low_lane < 20,
             jnp.where(low_lane < 10, pieces[0], pieces[1]),
             jnp.where(low_lane < 30, pieces[2], pieces[3]),
@@ -679,6 +684,31 @@
 
     for d in (2, 1, 3):
         begin(to_chip(d, x))
+
+    for d in range(1, 8):
+        to_z(d, (z + 8 - d) % 8).wait_recv()
+    local[9].wait()
+    down = [roll(zb5[i + 1], -32) if i < 8 else nothing8 for i in range(0, 10, 2)]
+    rise = [nothing8] + [roll(zb5[i + 1], 32) for i in range(1, 8, 2)]
+    flat = [
+        jnp.where(lane8 < 96, down[j], down[j + 1]) + jnp.where(lane8 >= 32, rise[j + 1], rise[j]) for j in range(4)
+    ]
+    solved = solve(jnp.concatenate(flat, axis=1), ci[...])
+    p5[0] = nothing8
+    p5[5] = nothing8
+    for j in range(4):
+        p5[j + 1] = solved[:, 128 * j : 128 * j + 128]
+    odd = z % 2
+    lead = (z + odd) // 2
+    edge = 32 + 64 * odd
+    rb5[x] = jnp.where(lane8 < edge, roll(p5[lead], edge), roll(p5[lead + 1], edge))
+
+    def to_chip5(d, me):
+        peer = (me + d) % 4
+        return send(rb5.at[me], rb5.at[me], r5send.at[d - 1], r5recv.at[me], px=px, py=2 * peer + core)
+
+    for d in (2, 1, 3):
+        begin(to_chip5(d, x))
 
     before, after = eb[py, 0], eb[py + 2, 0]
     corner_before, corner_after = eb[py, 1], eb[py + 2, 1]
@@ -701,31 +731,6 @@
         p0[2 * b] = solved[:, :128]
         p0[2 * b + 1] = solved[:, 128:]
 
-    for d in range(1, 8):
-        to_z(d, (z + 8 - d) % 8).wait_recv()
-    local[9].wait()
-    down = [roll(zb5[i + 1], -32) if i < 8 else nothing8 for i in range(0, 10, 2)]
-    rise = [nothing8] + [roll(zb5[i + 1], 32) for i in range(1, 8, 2)]
-    flat = [
-        jnp.where(lane8 < 96, down[j], down[j + 1]) + jnp.where(lane8 >= 32, rise[j + 1], rise[j]) for j in range(4)
-    ]
-    solved = solve(jnp.concatenate(flat, axis=1), ci[...])
-    p5[0] = nothing8
-    p5[5] = nothing8
-    for j in range(4):
-        p5[j + 1] = solved[:, 128 * j : 128 * j + 128]
-    odd = z % 2
-    lead = (z + odd) // 2
-    edge = 32 + 64 * odd
-    rb5[x] = jnp.where(lane8 < edge, roll(p5[lead], edge), roll(p5[lead + 1], edge))
-
-    def to_chip5(d, me):
-        peer = (me + d) % 4
-        return send(rb5.at[me], rb5.at[me], r5send.at[d - 1], r5recv.at[me], px=px, py=2 * peer + core)
-
-    for d in (2, 1, 3):
-        begin(to_chip5(d, x))
-
     got_rows(*h_refs)
     for d in (-1, 0, 1):
 
@@ -743,11 +748,24 @@
     one = lifted(one, up[0:128, :])
     for d in range(1, 4):
         to_chip(d, (x + 4 - d) % 4).wait_recv()
-    back = [rb[:, t].reshape(32, 128) for t in range(4)]
-    two = [only(jnp.logical_and(lane >= 42 * u, lane < 42 * u + 34), back[h]) for h in range(2) for u in range(3)]
-    three = [only((lane // 32) == s, back[2]) for s in range(4)]
+    for side, there in ((0, has_left), (1, has_right)):
+
+        @pl.when(there)
+        def _(side=side):
+            for c in range(4):
+                to_near(1 - side, x, c).wait_recv()
+
+    back = [rb[:, t].reshape(32, 128) for t in range(3)]
+    outer = [nb[side].reshape(32, 128) for side in range(2)]
+
+    def slot(tile, first, count):
+        return only(jnp.logical_and(lane >= first, lane < first + count), tile)
+
+    two = [slot(outer[0], 0, 34)] + [slot(back[0], 42 * u, 34) for u in range(3)]
+    two += [slot(back[1], 84, 34), slot(outer[1], 0, 34)]
+    three = [slot(outer[0], 64, 18), slot(back[1], 32, 18), slot(back[1], 64, 18), slot(outer[1], 64, 18)]
     four = [
-        only(jnp.logical_and(lane >= 64 * h + 10 * b, lane < 64 * h + 10 * b + 10), back[3])
+        only(jnp.logical_and(lane >= 64 * h + 10 * b, lane < 64 * h + 10 * b + 10), back[2])
         for b in range(4)
         for h in range(2)
     ]
@@ -780,8 +798,15 @@
 
     for copy in sent:
         copy.wait_send()
-    for refs in (b_refs, g_refs, h2_refs, h_refs):
+    for refs in (b_refs, g_refs, h_refs):
         sent_rows(*refs)
+
+    for side, there in ((0, has_left), (1, has_right)):
+
+        @pl.when(there)
+        def _(side=side):
+            for c in range(4):
+                to_near(side, c, x).wait_send()
 
     @pl.when(has_beside)
     def _():
@@ -855,17 +880,17 @@
             small(2, 3),
             small(2, 6),
             small(2, 6),
-            small(2, 3),
-            small(2, 3),
-            small(4, 4),
-            small(4, 4),
+            small(2, 4),
+            small(2, 4),
+            small(4, 3),
+            small(4, 3),
             small(4),
             small(6),
             dma((20,)),
         ]
         + [
-            dma if n == 0 else dma((n,))
-            for n in (7, 8, 7, 8, 2, 2, 3, 8, 0, 0, 3, 4, 3, 4, 7, 8, 2, 2, 2, 2, 3, 3, 2, 2, 2, 2, 3, 4, 3, 4)
+            dma if n == 0 else dma(n if isinstance(n, tuple) else (n,))
+            for n in (7, 8, 7, 8, 2, 2, 3, 8, 0, 0, 3, 4, 3, 4, 7, 8, 2, 2, 2, 2, 3, 3, 2, 2, (2, 4), (2, 4), 3, 4, 3, 4)
         ]
         + [pltpu.SemaphoreType.REGULAR((3,))],
         compiler_params=pltpu.CompilerParams(

time: 26.1 us -> 25.8 us (0.989); the launches traced: 26 us -> 25.4 us
  Pallas kernels: 25.3 us -> 24.7 us
    pallas_call x1, Pallas kernels: 25.3 us -> 24.7 us  [per_device(): pl.pallas_call(functools.partial(kernel, down_used, up_used), out_shape=j...]
where the time goes in v4:
time: 25.8 us; the launch traced here: 25.4 us
  Pallas kernels  24.7 us (96%)
  local copies, waits for them, and re-layouts  0.71 us (3%)
    pallas_call x1, Pallas kernels, per_device(): pl.pallas_call(functools.partial(kernel, down_used, up_used), out_shape=j...  24.7 us
    unnamed x1, local copies, waits for them, and re-layouts  0.71 us

profile of v4, /device:TPU:32, one launch (start us, length us, event | category | flops | bytes accessed | tf_op | source)
XLA Modules:
  0.0 25.4 jit_solution(14199569331700794217)
XLA Ops:
  0.0 24.7 %shard_map.109 = f32[512,128]{1,0:T(8,128)S(1)} custom-call(f32[512,128]{1,0:T(8,128)} %bitcast.3, bf16[8,1,520,256]{3,2,1,0:T(8,128)(2,1)} %ff_hbm.1, bf16[4,4,520,256]{3,2,1,0:T(8,128)(2,1)} %f1_hbm.1, bf16[2,2,520,256]{3,2,1,0:T(8,128)(2,1)} %f2_hbm.1, bf16[1,1,520,256]{3,2,1,0:T(8,128)(2,1)} %f3_hbm.1, bf16[16,1,264,128]{3,2,1,0:T(8,128)(2,1)} %f4_hbm.1, ...), custom_call_target="tpu_custom_call" | custom-call | tf_op jit(solution)/shard_map/pallas_call | solution.py:841
  24.7 0.7 %copy.13 = f32[32,16,128]{2,1,0:T(8,128)} copy(f32[32,16,128]{2,1,0:T(8,128)S(1)} %bitcast.2) | data formatting | bytes 524288

commit v5 on v4

--- a/solution.py
+++ b/solution.py
@@ -339,10 +339,6 @@
         for c in range(4):
             abuf[c, t - 1] = tile[8 * c : 8 * c + 8]
     a3[py] = abuf[x]
-    for d in FAR:
-        begin(to_three(d, py))
-    pl.semaphore_wait(zs.at[0], 2)
-    pass_on(1)
     for t in range(4, 9):
         own[t - 1] = packed(t)
     sb[0, 0] = own[0]
@@ -387,6 +383,10 @@
 
     b_refs = (sb, pb, bsend, brecv)
     start_rows(*b_refs)
+    for d in FAR:
+        begin(to_three(d, py))
+    pl.semaphore_wait(zs.at[0], 2)
+    pass_on(1)
     pl.semaphore_wait(zs.at[1], 2)
     pass_on(2)
 

time: 25.8 us -> 25.5 us (0.988); the launches traced: 25.4 us -> 25.4 us
  no operation moved by 1% of the time
where the time goes in v5:
time: 25.5 us; the launch traced here: 25.4 us
  Pallas kernels  24.7 us (97%)
  local copies, waits for them, and re-layouts  0.71 us (3%)
    pallas_call x1, Pallas kernels, per_device(): pl.pallas_call(functools.partial(kernel, down_used, up_used), out_shape=j...  24.7 us
    unnamed x1, local copies, waits for them, and re-layouts  0.71 us

profile of v5, /device:TPU:32, one launch (start us, length us, event | category | flops | bytes accessed | tf_op | source)
XLA Modules:
  0.0 25.4 jit_solution(10825005107420498060)
XLA Ops:
  0.0 24.7 %shard_map.109 = f32[512,128]{1,0:T(8,128)S(1)} custom-call(f32[512,128]{1,0:T(8,128)} %bitcast.3, bf16[8,1,520,256]{3,2,1,0:T(8,128)(2,1)} %ff_hbm.1, bf16[4,4,520,256]{3,2,1,0:T(8,128)(2,1)} %f1_hbm.1, bf16[2,2,520,256]{3,2,1,0:T(8,128)(2,1)} %f2_hbm.1, bf16[1,1,520,256]{3,2,1,0:T(8,128)(2,1)} %f3_hbm.1, bf16[16,1,264,128]{3,2,1,0:T(8,128)(2,1)} %f4_hbm.1, ...), custom_call_target="tpu_custom_call" | custom-call | tf_op jit(solution)/shard_map/pallas_call | solution.py:841
  24.7 0.7 %copy.13 = f32[32,16,128]{2,1,0:T(8,128)} copy(f32[32,16,128]{2,1,0:T(8,128)S(1)} %bitcast.2) | data formatting | bytes 524288
